TPU v7x, 128 devices: a whole 4x4x4 slice. The times are simulated.
128 devices in a mesh: grp: 4 (over x), sub: 32 (over z, y, core).
Axes of the slice: x: 4, y: 4, z: 4, core: 2. Of those that a mesh axis runs over, the one named last changes fastest.
Arguments:
- vectors: bfloat16 [128, 262144], P(None, ('grp', 'sub')), may hold values from -6 to 6
- geometry: bfloat16 [4, 262144], P(None, ('grp', 'sub')), may hold values from 0 to 4, as said below
- transfer: float32 [2, 4, 4, 512], P(None, 'grp'), may hold values from -6 to 6
Outputs:
- ortho_basis: float32 [128, 262144], P(None, ('grp', 'sub'))
- r_factor: float32 [128, 128], replicated
Inputs may be any that keep to these rules, and one draw needn't show every extreme that they name: `geometry`: rows 0 to 2 lie in the unit box, row 3 is positive and at least 0.25.
All inputs are finite; a program needn't handle non-finite values.
Results may differ from a plain program's by a relative error of at most 0.0065.
Values may be sent and summed in bfloat16 or wider, within the bound.
A program may use at most 128 MiB of HBM per device.

v0:
```python
import math

import jax
import jax.numpy as jnp
from jax import lax
from jax.sharding import PartitionSpec as P

KWAVE = 20.0
DELTA = 0.25
GOLDEN = math.pi * (3.0 - math.sqrt(5.0))


def extended(array, sides, width):
    for axis, dim in sides:
        size, length = (lax.axis_size(axis), array.shape[dim])
        up = [(i, (i + 1) % size) for i in range(size - 1)]
        down = [(j, i) for i, j in up]
        last = lax.slice_in_dim(array, length - width, length, axis=dim)
        leading = lax.slice_in_dim(array, 0, width, axis=dim)
        before = lax.ppermute(last, axis, up)
        after = lax.ppermute(leading, axis, down)
        array = jnp.concatenate([before, array, after], axis=dim)
    return array


def partner_2(block, axis, apart):
    count = lax.axis_size(axis)
    route = []
    for low in range(count):
        high = low | 1 << apart
        if high != low and high < count:
            route += [(low, high), (high, low)]
    return lax.ppermute(block, axis, route)


def kernel_tables(target, source, offsets):
    target_f = target.astype(jnp.float32)
    source_f = source.astype(jnp.float32)
    diff_x = target_f[0][None, :] - source_f[0][:, None] - offsets[:, None]
    diff_y = target_f[1][None, :] - source_f[1][:, None]
    diff_z = target_f[2][None, :] - source_f[2][:, None]
    dist_sq = diff_x * diff_x + diff_y * diff_y + diff_z * diff_z
    spread = source_f[3][:, None] / jnp.sqrt(dist_sq + DELTA * DELTA)
    phases = KWAVE * jnp.sqrt(dist_sq)
    return (
        (spread * jnp.cos(phases)).astype(jnp.bfloat16),
        (spread * jnp.sin(phases)).astype(jnp.bfloat16),
    )


def near_field(source_vec, source_geo, offsets, target_geo):
    half_cols = source_vec.shape[0] // 2
    panel_count = target_geo.shape[1]
    block_cols = min(512, panel_count)
    pieces = []
    for column in range(0, panel_count, block_cols):
        real_k, imag_k = kernel_tables(
            target_geo[:, column : column + block_cols], source_geo, offsets
        )
        part_a = jnp.dot(source_vec, real_k, preferred_element_type=jnp.float32)
        part_b = jnp.dot(source_vec, imag_k, preferred_element_type=jnp.float32)
        pieces.append(
            jnp.concatenate(
                (part_a[:half_cols] - part_b[half_cols:], part_a[half_cols:] + part_b[:half_cols]),
                0,
            )
        )
    return jnp.concatenate(pieces, 1)


def directions(dir_count):
    serial = jnp.arange(dir_count).astype(jnp.float32)
    height = 1.0 - (2.0 * serial + 1.0) / dir_count
    radius = jnp.sqrt(jnp.maximum(1.0 - height * height, 0.0))
    azimuth = serial * GOLDEN
    return (radius * jnp.cos(azimuth), radius * jnp.sin(azimuth), height)


def far_tables(geo, dir_count):
    points = geo.astype(jnp.float32)
    dir_x, dir_y, dir_z = directions(dir_count)
    phases = KWAVE * (
        dir_x[:, None] * points[0][None, :]
        + dir_y[:, None] * points[1][None, :]
        + dir_z[:, None] * points[2][None, :]
    )
    cos_table = jnp.cos(phases)
    sin_table = jnp.sin(phases)
    weight = points[3][None, :]
    return (
        (weight * cos_table).astype(jnp.bfloat16),
        (weight * sin_table).astype(jnp.bfloat16),
        cos_table.astype(jnp.bfloat16),
        sin_table.astype(jnp.bfloat16),
    )


def merge_pair(lower_fac, partner):
    contract = (((1,), (1,)), ((), ()))
    summed = lax.dot_general(
        lower_fac,
        lower_fac,
        contract,
        precision=lax.Precision.HIGHEST,
        preferred_element_type=jnp.float32,
    )
    summed = summed + lax.dot_general(
        partner,
        partner,
        contract,
        precision=lax.Precision.HIGHEST,
        preferred_element_type=jnp.float32,
    )
    return jnp.linalg.cholesky(summed)


def make_translate(tran_re, tran_im, half_cols):

    def translate(running, shard_piece, anchor):
        coef_re = tran_re[:, None, :]
        coef_im = tran_im[:, None, :]
        mom_re = shard_piece[:, :half_cols]
        mom_im = shard_piece[:, half_cols:]
        add_re = jnp.sum(coef_re * mom_re - coef_im * mom_im, axis=0)
        add_im = jnp.sum(coef_re * mom_im + coef_im * mom_re, axis=0)
        return jnp.concatenate((add_re, add_im), 0)

    return translate


def shards(vectors, geometry, transfer):
    half_cols = vectors.shape[0] // 2
    panel_count = vectors.shape[1]
    dir_count = transfer.shape[-1]
    sub_size = lax.axis_size("sub")
    grp_size = lax.axis_size("grp")
    contract = (((1,), (1,)), ((), ()))
    unit_row = jnp.ones((panel_count,), jnp.float32)
    joined = jnp.concatenate((vectors, geometry), 0)
    wide_rows = extended(joined, (("sub", 1),), panel_count)
    offsets = jnp.concatenate((-unit_row, 0.0 * unit_row, unit_row))
    near_part = near_field(
        wide_rows[: 2 * half_cols], wide_rows[2 * half_cols :], offsets, geometry
    )
    src_cos, src_sin, eval_cos, eval_sin = far_tables(geometry, dir_count)
    part_x = lax.dot_general(vectors, src_cos, contract, preferred_element_type=jnp.float32)
    part_z = lax.dot_general(vectors, src_sin, contract, preferred_element_type=jnp.float32)
    moment_scale = (panel_count * sub_size) ** (-0.5)
    moment = (
        jnp.concatenate(
            (part_x[:half_cols] + part_z[half_cols:], part_x[half_cols:] - part_z[:half_cols]), 0
        )
        * moment_scale
    )
    group_sum = lax.psum(moment, "sub")
    translate = make_translate(transfer[0, 0], transfer[1, 0], half_cols)
    local_exp = translate(
        jnp.zeros_like(group_sum),
        lax.all_gather(group_sum[None], "grp", axis=0, tiled=True),
        jnp.int32(0),
    )
    local_exp = local_exp.astype(jnp.bfloat16)
    part_a = jnp.dot(local_exp, eval_cos, preferred_element_type=jnp.float32)
    part_b = jnp.dot(local_exp, eval_sin, preferred_element_type=jnp.float32)
    far_part = jnp.concatenate(
        (part_a[:half_cols] - part_b[half_cols:], part_a[half_cols:] + part_b[:half_cols]), 0
    )
    near_scale = (3 * panel_count) ** (-0.5)
    far_scale = (dir_count * grp_size) ** (-0.5)
    applied = (
        0.5 * vectors.astype(jnp.float32) + near_scale * near_part + far_scale * far_part
    ).astype(jnp.bfloat16)
    inv_total = 1.0 / (panel_count * sub_size * grp_size)
    gram_mat = (
        lax.dot_general(applied, applied, contract, preferred_element_type=jnp.float32) * inv_total
    )
    lower_fac = jnp.linalg.cholesky(gram_mat)
    for level in range(sub_size.bit_length() - 1):
        partner = partner_2(lower_fac.astype(jnp.bfloat16), "sub", level).astype(lower_fac.dtype)
        lower_fac = merge_pair(lower_fac, partner)
    for level in range(grp_size.bit_length() - 1):
        partner = partner_2(lower_fac.astype(jnp.bfloat16), "grp", level).astype(lower_fac.dtype)
        lower_fac = merge_pair(lower_fac, partner)
    ortho_basis = lax.linalg.triangular_solve(
        lower_fac, applied.astype(jnp.float32), left_side=True, lower=True
    )
    return (ortho_basis, lower_fac.T)


def solution(mesh):
    in_specs = (P(None, ("grp", "sub")), P(None, ("grp", "sub")), P(None, "grp", None, None))
    out_specs = (P(None, ("grp", "sub")), P())
    return jax.shard_map(shards, mesh=mesh, in_specs=in_specs, out_specs=out_specs, check_vma=False)
```

profile of v0, /device:TPU:24, one launch (start us, length us, event | category | flops | bytes accessed | tf_op | source)
XLA Modules:
  0.0 758.0 jit_solution(7767568248212459756)
XLA Ops:
  14.3 18.9 %fusion.18 = f32[128,512]{1,0:T(8,128)S(1)} fusion(bf16[128,2048]{1,0:T(8,128)(2,1)} %param.4, f32[2048]{0:T(1024)S(1)} %bitcast.128, f32[512]{0:T(512)S(1)} %multiply_subtract_fusion, f32[2048]{0:T(1024)S(1)} %bitcast.124, f32[512]{0:T(512)S(1)} %get-tuple-element.55, f32[2048]{0:T(1024)S(1)} %bitcast.120, f32[512]{0:T(512)S(1)} %get-tuple-element.56, ...), kind=kOutput, calls=%fused_computation.40 | convolution fusion | flops 276824064 | bytes 825344 | tf_op jit(solution)/shard_map/dot_general | solution.py:147
  33.2 17.5 %fusion.19 = f32[128,512]{1,0:T(8,128)S(1)} fusion(bf16[128,2048]{1,0:T(8,128)(2,1)S(1)} %copy-done, f32[2048]{0:T(1024)S(1)} %bitcast.129, f32[512]{0:T(512)S(1)} %multiply_subtract_fusion, f32[2048]{0:T(1024)S(1)} %bitcast.125, f32[512]{0:T(512)S(1)} %get-tuple-element.55, f32[2048]{0:T(1024)S(1)} %bitcast.121, f32[512]{0:T(512)S(1)} %get-tuple-element.56, ...), kind=kOutput, calls=%fused_computation.41 | convolution fusion | flops 276824064 | bytes 825344 | tf_op jit(solution)/shard_map/dot_general | solution.py:146
  51.6 106.9 %all-reduce.2.cloned.1.call-done = f32[1,128,512]{2,1,0:T(8,128)} async-done(((f32[1,128,512]{2,1,0:T(8,128)}), f32[1,128,512]{2,1,0:T(8,128)}) %all-reduce.2.cloned.1.call-update) | async-done | bytes 262160 | tf_op jit(solution)/shard_map/psum | solution.py:155
  159.4 51.7 %fusion.5 = f32[128,512]{1,0:T(8,128)S(1)} fusion(f32[512]{0:T(512)S(1)} %bitcast.154, f32[512]{0:T(512)S(1)} %bitcast.156, f32[512]{0:T(512)S(1)} %bitcast.152, f32[6144]{0:T(1024)S(1)} %bitcast.96, f32[6144]{0:T(1024)S(1)} %bitcast.104, f32[6144]{0:T(1024)S(1)} %copy-done.3, f32[6144]{0:T(1024)S(1)} %bitcast.112, f32[6144]{0:T(1024)S(1)} %bitcast.88, ...), kind=kOutput, calls=%fused_computation.25 | convolution fusion | flops 849346560 | bytes 1964032 | tf_op jit(solution)/shard_map/dot_general | solution.py:61
  211.1 50.7 %fusion.4 = f32[128,512]{1,0:T(8,128)S(1)} fusion(f32[512]{0:T(512)S(1)} %bitcast.155, f32[512]{0:T(512)S(1)} %bitcast.157, f32[512]{0:T(512)S(1)} %bitcast.153, f32[6144]{0:T(1024)S(1)} %bitcast.97, f32[6144]{0:T(1024)S(1)} %bitcast.105, f32[6144]{0:T(1024)S(1)} %copy-done.3, f32[6144]{0:T(1024)S(1)} %bitcast.113, f32[6144]{0:T(1024)S(1)} %bitcast.89, ...), kind=kOutput, calls=%fused_computation.24 | convolution fusion | flops 849346560 | bytes 1964032 | tf_op jit(solution)/shard_map/dot_general | solution.py:60
  261.9 51.7 %fusion.3 = f32[128,512]{1,0:T(8,128)S(1)} fusion(f32[512]{0:T(512)S(1)} %bitcast.148, f32[512]{0:T(512)S(1)} %bitcast.146, f32[512]{0:T(512)S(1)} %bitcast.150, f32[6144]{0:T(1024)S(1)} %bitcast.98, f32[6144]{0:T(1024)S(1)} %bitcast.106, f32[6144]{0:T(1024)S(1)} %copy-done.3, f32[6144]{0:T(1024)S(1)} %bitcast.114, f32[6144]{0:T(1024)S(1)} %bitcast.90, ...), kind=kOutput, calls=%fused_computation.23 | convolution fusion | flops 849346560 | bytes 1964032 | tf_op jit(solution)/shard_map/dot_general | solution.py:61
  313.6 50.7 %fusion.2 = f32[128,512]{1,0:T(8,128)S(1)} fusion(f32[512]{0:T(512)S(1)} %bitcast.149, f32[512]{0:T(512)S(1)} %bitcast.147, f32[512]{0:T(512)S(1)} %bitcast.151, f32[6144]{0:T(1024)S(1)} %bitcast.99, f32[6144]{0:T(1024)S(1)} %bitcast.107, f32[6144]{0:T(1024)S(1)} %copy-done.3, f32[6144]{0:T(1024)S(1)} %bitcast.115, f32[6144]{0:T(1024)S(1)} %bitcast.91, ...), kind=kOutput, calls=%fused_computation.22 | convolution fusion | flops 849346560 | bytes 1964032 | tf_op jit(solution)/shard_map/dot_general | solution.py:60
  364.3 51.7 %fusion.1 = f32[128,512]{1,0:T(8,128)S(1)} fusion(f32[6144]{0:T(1024)S(1)} %bitcast.100, f32[512]{0:T(512)S(1)} %bitcast.142, f32[6144]{0:T(1024)S(1)} %bitcast.108, f32[512]{0:T(512)S(1)} %bitcast.144, f32[6144]{0:T(1024)S(1)} %copy-done.3, f32[6144]{0:T(1024)S(1)} %bitcast.116, f32[512]{0:T(512)S(1)} %bitcast.140, f32[6144]{0:T(1024)S(1)} %bitcast.92, ...), kind=kOutput, calls=%fused_computation.21 | convolution fusion | flops 849346560 | bytes 1964032 | tf_op jit(solution)/shard_map/dot_general | solution.py:61
  416.0 50.7 %fusion = f32[128,512]{1,0:T(8,128)S(1)} fusion(f32[6144]{0:T(1024)S(1)} %bitcast.101, f32[512]{0:T(512)S(1)} %bitcast.143, f32[6144]{0:T(1024)S(1)} %bitcast.109, f32[512]{0:T(512)S(1)} %bitcast.145, f32[6144]{0:T(1024)S(1)} %copy-done.3, f32[6144]{0:T(1024)S(1)} %bitcast.117, f32[512]{0:T(512)S(1)} %bitcast.141, f32[6144]{0:T(1024)S(1)} %bitcast.93, ...), kind=kOutput, calls=%fused_computation.20 | convolution fusion | flops 849346560 | bytes 1964032 | tf_op jit(solution)/shard_map/dot_general | solution.py:60
  466.8 51.1 %fusion.6 = f32[128,512]{1,0:T(8,128)S(1)} fusion(f32[512]{0:T(512)S(1)} %bitcast.136, f32[512]{0:T(512)S(1)} %bitcast.134, f32[512]{0:T(512)S(1)} %bitcast.138, f32[6144]{0:T(1024)S(1)} %bitcast.102, f32[6144]{0:T(1024)S(1)} %bitcast.110, f32[6144]{0:T(1024)S(1)} %copy-done.3, f32[6144]{0:T(1024)S(1)} %bitcast.118, f32[6144]{0:T(1024)S(1)} %bitcast.94, ...), kind=kOutput, calls=%fused_computation.26 | convolution fusion | flops 849346560 | bytes 1964032 | tf_op jit(solution)/shard_map/dot_general | solution.py:60
  517.9 51.7 %fusion.7 = f32[128,512]{1,0:T(8,128)S(1)} fusion(f32[512]{0:T(512)S(1)} %bitcast.137, f32[512]{0:T(512)S(1)} %bitcast.135, f32[512]{0:T(512)S(1)} %bitcast.139, f32[6144]{0:T(1024)S(1)} %bitcast.103, f32[6144]{0:T(1024)S(1)} %bitcast.111, f32[6144]{0:T(1024)S(1)} %copy-done.3, f32[6144]{0:T(1024)S(1)} %bitcast.119, f32[6144]{0:T(1024)S(1)} %bitcast.95, ...), kind=kOutput, calls=%fused_computation.27 | convolution fusion | flops 849346560 | bytes 1964032 | tf_op jit(solution)/shard_map/dot_general | solution.py:61
  571.1 14.7 %fusion.14 = f32[128,2048]{1,0:T(8,128)S(1)} fusion(f32[2048]{0:T(1024)S(1)} %bitcast.130, f32[512]{0:T(512)S(1)} %multiply_subtract_fusion, f32[2048]{0:T(1024)S(1)} %bitcast.126, f32[512]{0:T(512)S(1)} %get-tuple-element.55, f32[2048]{0:T(1024)S(1)} %bitcast.122, f32[512]{0:T(512)S(1)} %get-tuple-element.56, bf16[64,512]{1,0:T(8,128)(2,1)S(1)} %get-tuple-element.8, ...), kind=kOutput, calls=%fused_computation.36 | convolution fusion | flops 276037632 | bytes 1210368 | tf_op jit(solution)/shard_map/dot_general | solution.py:163
  585.7 14.8 %fusion.12 = f32[128,2048]{1,0:T(8,128)S(1)} fusion(f32[2048]{0:T(1024)S(1)} %bitcast.131, f32[512]{0:T(512)S(1)} %multiply_subtract_fusion, f32[2048]{0:T(1024)S(1)} %bitcast.127, f32[512]{0:T(512)S(1)} %get-tuple-element.55, f32[2048]{0:T(1024)S(1)} %bitcast.123, f32[512]{0:T(512)S(1)} %get-tuple-element.56, bf16[64,512]{1,0:T(8,128)(2,1)S(1)} %get-tuple-element.8, ...), kind=kOutput, calls=%fused_computation.35 | convolution fusion | flops 276037632 | bytes 1210368 | tf_op jit(solution)/shard_map/dot_general | solution.py:164
  601.4 11.7 %cholesky.134 = f32[128,128]{1,0:T(8,128)S(1)} custom-call(f32[128,128]{1,0:T(8,128)S(1)} %fusion.41), custom_call_target="Cholesky" | custom-call | tf_op jit(solution)/shard_map/jit(cholesky)/cholesky | solution.py:177
  616.4 11.7 %cholesky.145 = f32[128,128]{1,0:T(8,128)S(1)} custom-call(f32[128,128]{1,0:T(8,128)S(1)} %fusion.40), custom_call_target="Cholesky" | custom-call | tf_op jit(solution)/shard_map/jit(cholesky)/cholesky | solution.py:114
  633.7 11.7 %cholesky.156 = f32[128,128]{1,0:T(8,128)S(1)} custom-call(f32[128,128]{1,0:T(8,128)S(1)} %fusion.39), custom_call_target="Cholesky" | custom-call | tf_op jit(solution)/shard_map/jit(cholesky)/cholesky | solution.py:114
  648.1 4.4 collective-permute-done.4
  652.7 11.7 %cholesky.167 = f32[128,128]{1,0:T(8,128)S(1)} custom-call(f32[128,128]{1,0:T(8,128)S(1)} %fusion.38), custom_call_target="Cholesky" | custom-call | tf_op jit(solution)/shard_map/jit(cholesky)/cholesky | solution.py:114
  670.0 11.7 %cholesky.178 = f32[128,128]{1,0:T(8,128)S(1)} custom-call(f32[128,128]{1,0:T(8,128)S(1)} %fusion.37), custom_call_target="Cholesky" | custom-call | tf_op jit(solution)/shard_map/jit(cholesky)/cholesky | solution.py:114
  684.5 4.3 collective-permute-done.6
  689.1 11.7 %cholesky.189 = f32[128,128]{1,0:T(8,128)S(1)} custom-call(f32[128,128]{1,0:T(8,128)S(1)} %fusion.36), custom_call_target="Cholesky" | custom-call | tf_op jit(solution)/shard_map/jit(cholesky)/cholesky | solution.py:114
  706.4 11.7 %cholesky.200 = f32[128,128]{1,0:T(8,128)S(1)} custom-call(f32[128,128]{1,0:T(8,128)S(1)} %fusion.35), custom_call_target="Cholesky" | custom-call | tf_op jit(solution)/shard_map/jit(cholesky)/cholesky | solution.py:114
  725.5 11.7 %cholesky.211 = f32[128,128]{1,0:T(8,128)S(1)} custom-call(f32[128,128]{1,0:T(8,128)S(1)} %fusion.34), custom_call_target="Cholesky" | custom-call | tf_op jit(solution)/shard_map/jit(cholesky)/cholesky | solution.py:114
  739.3 9.8 %custom-call.5 = f32[1,128,128]{1,2,0:T(8,128)S(1)} custom-call(f32[1,128,128]{2,1,0:T(8,128)S(1)} %get-tuple-element.26), custom_call_target="InvertDiagBlocksLowerTriangular" | custom-call | tf_op jit(solution)/shard_map/triangular_solve | solution.py:184
  (107 shorter events, 48.1 us)
Async XLA Ops:
  7.2 151.4 %all-reduce.2.cloned.1.call-start = ((), (), s32[]{:S(2)}) async-start(), calls=%async_computation | async-start | bytes 524288 | tf_op jit(solution)/shard_map/psum | solution.py:155
  9.0 149.5 %collective-permute-start.1 = (bf16[132,2048]{1,0:T(8,128)(2,1)S(1)}, bf16[132,2048]{1,0:T(8,128)(2,1)S(1)}, u32[]{:S(2)}, u32[]{:S(2)}) collective-permute-start(bf16[132,2048]{1,0:T(8,128)(2,1)S(1)} %constant_dynamic-update-slice_fusion), channel_id=1, source_target_pairs={{1,0},{2,1},{3,2},{4,3},{5,4},{6,5},{7,6},{8,7},{9,8},{10,9},{11,1... | collective-permute-start | bytes 1622024 | tf_op jit(solution)/shard_map/ppermute | solution.py:21
  11.1 147.5 %collective-permute-start = (bf16[132,2048]{1,0:T(8,128)(2,1)S(1)}, bf16[132,2048]{1,0:T(8,128)(2,1)S(1)}, u32[]{:S(2)}, u32[]{:S(2)}) collective-permute-start(bf16[132,2048]{1,0:T(8,128)(2,1)S(1)} %constant_dynamic-update-slice_fusion), channel_id=1, source_target_pairs={{0,1},{1,2},{2,3},{3,4},{4,5},{5,6},{6,7},{7,8},{8,9},{9,10},{10,1... | collective-permute-start | bytes 1622024 | tf_op jit(solution)/shard_map/ppermute | solution.py:20
  14.3 18.9 %copy-start = (bf16[128,2048]{1,0:T(8,128)(2,1)S(1)}, bf16[128,2048]{1,0:T(8,128)(2,1)}, u32[]{:S(2)}) copy-start(bf16[128,2048]{1,0:T(8,128)(2,1)} %param.4) | copy-start | bytes 1572868
  33.2 18.3 %copy-start.1 = (bf16[4,2048]{1,0:T(4,128)(2,1)S(1)}, bf16[4,2048]{1,0:T(4,128)(2,1)}, u32[]{:S(2)}) copy-start(bf16[4,2048]{1,0:T(4,128)(2,1)} %param.5) | copy-start | bytes 49156
  50.7 0.9 copy-start.2
  51.5 518.2 %all-gather.2.cloned.1.call-start = ((), (), s32[]{:S(2)}) async-start(), calls=%async_computation.1 | async-start | bytes 1310720 | tf_op jit(solution)/shard_map/all_gather | solution.py:159
  158.7 0.7 copy-start.3
  614.4 1.7 collective-permute-start.2
  629.4 4.0 collective-permute-start.3
  646.8 5.7 collective-permute-start.4
  665.8 4.0 collective-permute-start.5
  683.1 5.7 collective-permute-start.6
  702.1 4.0 collective-permute-start.7
  719.5 5.8 collective-permute-start.8
Sparse Core Ops, SparseCore 0:
  51.6 106.8 all-reduce.1
  160.3 22.7 all-gather.1
where the time goes:
time: 767 us; the launch traced here: 758 us
  matrix products  485 us (63%)
  waiting for transfers between devices  125 us (16%)
  other arithmetic  117 us (15%)
  between operations  15 us (2%)
  starting transfers between devices  10.8 us (1%)
    dot_general x4, matrix products, near_field(): part_b = jnp.dot(source_vec, imag_k, preferred_element_type=jnp.float32)  207 us
    dot_general x4, matrix products, near_field(): part_a = jnp.dot(source_vec, real_k, preferred_element_type=jnp.float32)  203 us
    psum x1, waiting for transfers between devices, shards(): group_sum = lax.psum(moment, 'sub')  107 us
    another operation x21, other arithmetic, merge_pair(): return jnp.linalg.cholesky(summed)  86.7 us
    dot_general x1, matrix products, shards(): lax.dot_general(vectors, src_sin, contract, preferred_element_type=jnp.fl...  18.9 us
    ppermute x7, waiting for transfers between devices, partner_2(): return lax.ppermute(block, axis, route)  18 us
    dot_general x1, matrix products, shards(): lax.dot_general(vectors, src_cos, contract, preferred_element_type=jnp.fl...  17.5 us
  transfers between devices with their start and end apart: 11, of which 8 were waited for; matrix products, arithmetic and copies ran while one was open for 60% of the time, Pallas kernels for 0%

commit v1 on v0

v1 whole, which is shorter than its diff:
```python
import functools
import math

import jax
import jax.numpy as jnp
import numpy as np
from jax import lax
from jax.experimental import pallas as pl
from jax.experimental.pallas import tpu as pltpu
from jax.sharding import PartitionSpec as P

F32 = jnp.float32
BF16 = jnp.bfloat16
MESH = pl.DeviceIdType.MESH

KWAVE = 20.0
DELTA = 0.25
GOLDEN = math.pi * (3.0 - math.sqrt(5.0))
TURN = KWAVE / (2.0 * math.pi)
SOFT = DELTA * DELTA * TURN * TURN
Q0 = -1.03910273
P0, P1, P2 = -0.33076115, 1.40669993, -0.3346358
MAGIC = 1.5 * 2.0**23

TILE = 512
ROWS = 64
NT = (((1,), (1,)), ((), ()))
TN = (((0,), (0,)), ((), ()))


def half_angle(t):
    f = t - ((t + MAGIC) - MAGIC)
    u = f * f
    return (P2 * u + P1) * u + P0, f * (u + Q0)


def rotated(x, axis):
    half = x.shape[axis] // 2
    re = lax.slice_in_dim(x, 0, half, axis=axis)
    im = lax.slice_in_dim(x, half, 2 * half, axis=axis)
    return jnp.concatenate((-im, re), axis)


def lane_rotated(x):
    half = x.shape[-1] // 2
    lane = lax.broadcasted_iota(jnp.int32, x.shape, x.ndim - 1)
    turned = pltpu.roll(x, half, x.ndim - 1)
    return jnp.where(lane < half, -turned, turned)


def remote(src, dst, send_sem, recv_sem, device):
    return pltpu.make_async_remote_copy(
        src_ref=src,
        dst_ref=dst,
        send_sem=send_sem,
        recv_sem=recv_sem,
        device_id=device,
        device_id_type=MESH,
    )


def product_kernel(
    n_grp, n_sub,
    vec, geo, tran, dirs, sel,
    applied, gram,
    wv, wv_nb, geo_nb, tables, moment, mom_recv, grp_src, grp_recv, tran_t, loc, loc_mat,
    xrep, yrep, w2, g, acc, q, z_send, z_recv,
    gram_src, gram_recv, gsum_recv, gram_all,
    halo_s, halo_r, mom_s, mom_r, grp_s, grp_r, loc_s, loc_r, z_s, z_r,
    gr_s, gr_r, gg_s, gg_r, ga_s, ga_r,
):
    cols, panels = vec.shape
    dir_count = dirs.shape[0]
    chunk = dir_count // n_sub
    n_tiles = panels // TILE
    me_s = lax.axis_index("sub")
    me_g = lax.axis_index("grp")
    has_right = me_s < n_sub - 1
    has_left = me_s > 0

    def peer(k):
        return lax.rem(me_s + k, n_sub)

    def peer_g(k):
        return lax.rem(me_g + k, n_grp)

    barrier = pltpu.get_barrier_semaphore()

    def greet(k, _):
        pl.semaphore_signal(barrier, inc=1, device_id={"sub": peer(k)}, device_id_type=MESH)
        return 0

    lax.fori_loop(1, n_sub, greet, 0)

    def greet_g(k, _):
        pl.semaphore_signal(barrier, inc=1, device_id={"grp": peer_g(k)}, device_id_type=MESH)
        return 0

    lax.fori_loop(1, n_grp, greet_g, 0)

    weight = geo[3:4, :].astype(F32)
    wv[...] = (vec[...].astype(F32) * weight).astype(BF16)

    pl.semaphore_wait(barrier, n_sub - 1 + n_grp - 1)

    def halo(dst_sub):
        return (
            remote(wv, wv_nb, halo_s.at[0], halo_r.at[0], {"sub": dst_sub}),
            remote(geo, geo_nb, halo_s.at[1], halo_r.at[1], {"sub": dst_sub}),
        )

    left = lax.rem(me_s + n_sub - 1, n_sub)
    right = lax.rem(me_s + 1, n_sub)

    @pl.when(has_left)
    def _():
        for copy in halo(left):
            copy.start()

    def far_tables(n, _):
        k = n // n_tiles
        col = pl.multiple_of((n % n_tiles) * TILE, TILE)
        turns = jnp.dot(
            dirs[pl.ds(pl.multiple_of(k * 128, 128), 128), :],
            geo[:, pl.ds(col, TILE)],
            preferred_element_type=F32,
        )
        a, b = half_angle(turns)
        aa, bb = a * a, b * b
        norm = aa + bb
        inv = lax.rsqrt(norm * norm)
        row = pl.multiple_of(k * 256, 256)
        tables[pl.ds(row, 128), pl.ds(col, TILE)] = ((aa - bb) * inv).astype(BF16)
        tables[pl.ds(row + 128, 128), pl.ds(col, TILE)] = (a * b * inv).astype(BF16)
        return 0

    lax.fori_loop(0, dir_count // 128 * n_tiles, far_tables, 0)

    moment_scale = (panels * n_sub) ** (-0.5)
    for k in range(dir_count // 128):
        both = lax.dot_general(
            tables[k * 256 : k * 256 + 256, :], wv[...], NT, preferred_element_type=F32
        )
        moment[k * 128 : k * 128 + 128, :] = (
            both[:128] - 2.0 * lane_rotated(both[128:])
        ) * moment_scale

    def rows_of(ref, i, size):
        return ref.at[pl.ds(pl.multiple_of(i * size, size), size), :]

    def send_moment(k, _):
        p = peer(k)
        remote(
            rows_of(moment, p, chunk), mom_recv.at[me_s], mom_s.at[p], mom_r.at[me_s], {"sub": p}
        ).start()
        return 0

    lax.fori_loop(1, n_sub, send_moment, 0)

    for k in range(3):
        xrep[k] = jnp.broadcast_to(geo[k : k + 1, :].astype(F32) * TURN, (8, panels))

    def source_side(geo_ref, wv_ref, base, offset):
        for k in range(3):
            def spread(n, _):
                col = pl.multiple_of(n * TILE, TILE)
                y = lax.dot_general(
                    geo_ref[:, pl.ds(col, TILE)], sel[:, k * 128 : k * 128 + 128], TN,
                    preferred_element_type=F32,
                )
                if k == 0 and offset:
                    y = y + float(offset)
                yrep[k, pl.ds(base + col, TILE), :] = y * TURN
                return 0
            lax.fori_loop(0, n_tiles, spread, 0)
        for n in range(panels // 128):
            block = wv_ref[:, n * 128 : n * 128 + 128].astype(F32)
            at = 2 * base + n * 256
            w2[:, at : at + 128] = block.astype(BF16)
            w2[:, at + 128 : at + 256] = (2.0 * rotated(block, 0)).astype(BF16)

    source_side(geo, wv, 0, 0)
    acc[...] = jnp.zeros_like(acc)

    def near_tile(source, target, symmetric):
        i0 = pl.multiple_of(target * TILE, TILE)

        def strip(r, _):
            for l in range(0, TILE, 128):
                for sub in range(0, ROWS, 16):
                    row = pl.multiple_of(source * TILE + r * ROWS, ROWS) + sub

                    def diff(k):
                        y = yrep[k, pl.ds(row, 16), :].reshape(2, 8, 128)
                        return xrep[k, :, pl.ds(pl.multiple_of(i0 + l, 128), 128)] - y

                    dx, dy, dz = diff(0), diff(1), diff(2)
                    d2 = dx * dx + dy * dy + dz * dz
                    d2e = d2 + 1e-30
                    a, b = half_angle(d2e * lax.rsqrt(d2e))
                    aa, bb = a * a, b * b
                    norm = aa + bb
                    inv = lax.rsqrt(norm * norm * (d2 + SOFT))
                    at = pl.multiple_of(
                        (r * ROWS) // 128 * 256 + lax.rem(r * ROWS, 128), ROWS
                    ) + sub
                    g[pl.ds(at, 16), l : l + 128] = (
                        ((aa - bb) * inv).reshape(16, 128).astype(BF16)
                    )
                    g[pl.ds(at + 128, 16), l : l + 128] = (
                        ((a * b) * inv).reshape(16, 128).astype(BF16)
                    )
            return 0

        lax.fori_loop(0, TILE // ROWS, strip, 0)
        acc[:, pl.ds(i0, TILE)] += jnp.dot(
            w2[:, pl.ds(pl.multiple_of(source * 2 * TILE, 2 * TILE), 2 * TILE)],
            g[...],
            preferred_element_type=F32,
        )
        if symmetric:
            q[...] += lax.dot_general(
                wv[:, pl.ds(i0, TILE)], g[...], NT, preferred_element_type=F32
            )

    def mirrored(n):
        re = q[:, n * 256 : n * 256 + 128]
        im = q[:, n * 256 + 128 : n * 256 + 256]
        return re + 2.0 * rotated(im, 0)

    def send_z(j):
        return remote(z_send.at[j], z_recv.at[j], z_s.at[j], z_r.at[j], {"sub": right})

    @pl.when(has_right)
    def _():
        for copy in halo(left):
            copy.wait_recv()
        source_side(geo_nb, wv_nb, panels, 1)

    def neighbour_block(j):
        @pl.when(has_right)
        def _():
            q[...] = jnp.zeros_like(q)

            def step(i, _):
                near_tile(n_tiles + j, i, True)
                return 0

            lax.fori_loop(0, n_tiles, step, 0)
            for n in range(TILE // 128):
                z_send[j, :, n * 128 : n * 128 + 128] = mirrored(n).astype(BF16)
            send_z(j).start()

    def own_block(j):
        near_tile(j, j, False)
        if j < n_tiles - 1:
            q[...] = jnp.zeros_like(q)

            def step(i, _):
                near_tile(j, i, True)
                return 0

            lax.fori_loop(j + 1, n_tiles, step, 0)
            for n in range(TILE // 128):
                at = j * TILE + n * 128
                acc[:, at : at + 128] += mirrored(n)

    def reduce_moment():
        def arrived(k, _):
            p = peer(k)
            remote(
                rows_of(moment, p, chunk), mom_recv.at[p], mom_s.at[p], mom_r.at[p], {"sub": p}
            ).wait()
            return 0

        mom_recv[me_s] = moment[pl.ds(pl.multiple_of(me_s * chunk, chunk), chunk), :]
        lax.fori_loop(1, n_sub, arrived, 0)
        total = mom_recv[0]
        for n in range(1, n_sub):
            total = total + mom_recv[n]
        grp_src[...] = total
        grp_recv[me_g] = total

        def send(k, _):
            p = peer_g(k)
            remote(grp_src, grp_recv.at[me_g], grp_s.at[p], grp_r.at[me_g], {"grp": p}).start()
            return 0

        lax.fori_loop(1, n_grp, send, 0)

    def translate():
        def arrived(k, _):
            p = peer_g(k)
            remote(grp_src, grp_recv.at[p], grp_s.at[p], grp_r.at[p], {"grp": p}).wait()
            return 0

        lax.fori_loop(1, n_grp, arrived, 0)
        for part in range(2):
            tran_t[:, part * n_grp : part * n_grp + n_grp] = tran[part, 0].T
        coef = tran_t[pl.ds(pl.multiple_of(me_s * chunk, chunk), chunk), :]
        total = jnp.zeros((chunk, cols), F32)
        for h in range(n_grp):
            m = grp_recv[h]
            total = total + coef[:, h : h + 1] * m
            total = total + coef[:, n_grp + h : n_grp + h + 1] * lane_rotated(m)
        loc[me_s] = total.astype(BF16)

        def send(k, _):
            p = peer(k)
            remote(loc.at[me_s], loc.at[me_s], loc_s.at[p], loc_r.at[me_s], {"sub": p}).start()
            return 0

        lax.fori_loop(1, n_sub, send, 0)

    neighbour_block(0)
    reduce_moment()
    neighbour_block(1)
    translate()
    for j in range(2, n_tiles):
        neighbour_block(j)
    for j in range(n_tiles):
        own_block(j)

    def loc_arrived(k, _):
        p = peer(k)
        remote(loc.at[me_s], loc.at[p], loc_s.at[p], loc_r.at[p], {"sub": p}).wait()
        return 0

    lax.fori_loop(1, n_sub, loc_arrived, 0)
    per = 128 // chunk
    for k in range(dir_count // 128):
        block = jnp.concatenate([loc[k * per + n].astype(F32) for n in range(per)], 0)
        loc_mat[:, k * 256 : k * 256 + 128] = block.T.astype(BF16)
        loc_mat[:, k * 256 + 128 : k * 256 + 256] = (2.0 * lane_rotated(block)).T.astype(BF16)

    @pl.when(has_left)
    def _():
        for copy in halo(left):
            copy.wait_send()
        for j in range(n_tiles):
            send_z(j).wait_recv()
            acc[:, j * TILE : j * TILE + TILE] += z_recv[j].astype(F32)

    @pl.when(has_right)
    def _():
        for j in range(n_tiles):
            send_z(j).wait_send()

    near_scale = TURN * (3 * panels) ** (-0.5)
    far_scale = (dir_count * n_grp) ** (-0.5)
    partial = jnp.zeros((cols, cols), F32)
    for j in range(n_tiles):
        at = slice(j * TILE, j * TILE + TILE)
        far = jnp.dot(loc_mat[...], tables[:, at], preferred_element_type=F32)
        tile = (
            0.5 * vec[:, at].astype(F32) + near_scale * acc[:, at] + far_scale * far
        ).astype(BF16)
        applied[:, at] = tile
        partial = partial + lax.dot_general(tile, tile, NT, preferred_element_type=F32)
    partial = partial * (1.0 / (panels * n_sub * n_grp))

    n_own = cols // 8
    stride = n_sub // n_own
    mine = me_s // stride
    owner = lax.rem(me_s, stride) == 0
    gram_src[...] = partial.reshape(n_own, 8, cols)

    def gram_copy(c, slot, sem):
        return remote(
            gram_src.at[c], gram_recv.at[slot], gr_s.at[c], gr_r.at[sem], {"sub": c * stride}
        )

    def send_gram(k, _):
        c = lax.rem(mine + k, n_own)
        gram_copy(c, me_s, me_s).start()
        return 0

    lax.fori_loop(1, n_own, send_gram, 0)

    @pl.when(jnp.logical_not(owner))
    def _():
        gram_copy(mine, me_s, me_s).start()

    @pl.when(owner)
    def _():
        gram_recv[me_s] = gram_src[mine]

        def arrived(k, _):
            p = peer(k)
            gram_copy(mine, p, p).wait_recv()
            return 0

        lax.fori_loop(1, n_sub, arrived, 0)
        total = gram_recv[0]
        for n in range(1, n_sub):
            total = total + gram_recv[n]
        gsum_recv[me_g] = total

        def swap(k, _):
            p = peer_g(k)
            remote(
                gsum_recv.at[me_g], gsum_recv.at[me_g], gg_s.at[p], gg_r.at[me_g], {"grp": p}
            ).start()
            return 0

        lax.fori_loop(1, n_grp, swap, 0)

        def swapped(k, _):
            p = peer_g(k)
            remote(
                gsum_recv.at[me_g], gsum_recv.at[p], gg_s.at[p], gg_r.at[p], {"grp": p}
            ).wait()
            return 0

        lax.fori_loop(1, n_grp, swapped, 0)
        total = gsum_recv[0]
        for n in range(1, n_grp):
            total = total + gsum_recv[n]
        gram_all[mine] = total

        def spread(k, _):
            p = peer(k)
            remote(
                gram_all.at[mine], gram_all.at[mine], ga_s.at[p], ga_r.at[mine], {"sub": p}
            ).start()
            return 0

        lax.fori_loop(1, n_sub, spread, 0)

    def gathered(k, _):
        c = lax.rem(mine + k, n_own)
        remote(
            gram_all.at[c], gram_all.at[c], ga_s.at[c], ga_r.at[c], {"sub": c * stride}
        ).wait_recv()
        return 0

    lax.fori_loop(1, n_own, gathered, 0)

    @pl.when(jnp.logical_not(owner))
    def _():
        remote(
            gram_all.at[mine], gram_all.at[mine], ga_s.at[mine], ga_r.at[mine],
            {"sub": mine * stride},
        ).wait_recv()
        gram_copy(mine, me_s, me_s).wait_send()

    def sent(k, _):
        gram_copy(lax.rem(mine + k, n_own), me_s, me_s).wait_send()
        return 0

    lax.fori_loop(1, n_own, sent, 0)

    @pl.when(owner)
    def _():
        def spread_sent(k, _):
            p = peer(k)
            remote(
                gram_all.at[mine], gram_all.at[mine], ga_s.at[p], ga_r.at[mine], {"sub": p}
            ).wait_send()
            return 0

        lax.fori_loop(1, n_sub, spread_sent, 0)

    gram[...] = gram_all[...].reshape(cols, cols)


def direction_table(count):
    serial = np.arange(count).astype(np.float32)
    height = (1.0 - (2.0 * serial.astype(np.float64) + 1.0) / count)
    radius = np.sqrt(np.maximum(1.0 - height * height, 0.0))
    azimuth = (serial * np.float32(GOLDEN)).astype(np.float64)
    unit = TURN * np.stack((radius * np.cos(azimuth), radius * np.sin(azimuth), height), 1)
    table = np.zeros((count, 16), np.float64)
    for part in range(3):
        piece = unit.astype(jnp.bfloat16).astype(np.float64)
        table[:, 4 * part : 4 * part + 3] = piece
        unit = unit - piece
    return table.astype(jnp.bfloat16)


def selectors():
    table = np.zeros((16, 3 * 128), np.float32)
    for k in range(3):
        table[k, k * 128 : k * 128 + 128] = 1.0
    return table.astype(jnp.bfloat16)


def shards(n_grp, n_sub, vectors, geometry, transfer):
    cols, panels = vectors.shape
    dir_count = transfer.shape[-1]
    chunk = dir_count // n_sub
    n_tiles = panels // TILE
    n_own = cols // 8
    geo = jnp.concatenate((geometry,) * 4, 0)
    dma = pltpu.SemaphoreType.DMA
    applied, gram = pl.pallas_call(
        functools.partial(product_kernel, n_grp, n_sub),
        out_shape=(
            jax.ShapeDtypeStruct((cols, panels), BF16),
            jax.ShapeDtypeStruct((cols, cols), F32),
        ),
        in_specs=[pl.BlockSpec(memory_space=pltpu.VMEM)] * 5,
        out_specs=[pl.BlockSpec(memory_space=pltpu.VMEM)] * 2,
        scratch_shapes=[
            pltpu.VMEM((cols, panels), BF16),
            pltpu.VMEM((cols, panels), BF16),
            pltpu.VMEM((16, panels), BF16),
            pltpu.VMEM((2 * dir_count, panels), BF16),
            pltpu.VMEM((dir_count, cols), F32),
            pltpu.VMEM((n_sub, chunk, cols), F32),
            pltpu.VMEM((chunk, cols), F32),
            pltpu.VMEM((n_grp, chunk, cols), F32),
            pltpu.VMEM((dir_count, 2 * n_grp), F32),
            pltpu.VMEM((n_sub, chunk, cols), BF16),
            pltpu.VMEM((cols, 2 * dir_count), BF16),
            pltpu.VMEM((3, 8, panels), F32),
            pltpu.VMEM((3, 2 * panels, 128), F32),
            pltpu.VMEM((cols, 4 * panels), BF16),
            pltpu.VMEM((2 * TILE, TILE), BF16),
            pltpu.VMEM((cols, panels), F32),
            pltpu.VMEM((cols, 2 * TILE), F32),
            pltpu.VMEM((n_tiles, cols, TILE), BF16),
            pltpu.VMEM((n_tiles, cols, TILE), BF16),
            pltpu.VMEM((n_own, 8, cols), F32),
            pltpu.VMEM((n_sub, 8, cols), F32),
            pltpu.VMEM((n_grp, 8, cols), F32),
            pltpu.VMEM((n_own, 8, cols), F32),
            dma((2,)), dma((2,)),
            dma((n_sub,)), dma((n_sub,)),
            dma((n_grp,)), dma((n_grp,)),
            dma((n_sub,)), dma((n_sub,)),
            dma((n_tiles,)), dma((n_tiles,)),
            dma((n_own,)), dma((n_sub,)),
            dma((n_grp,)), dma((n_grp,)),
            dma((n_sub,)), dma((n_own,)),
        ],
        compiler_params=pltpu.CompilerParams(
            collective_id=0, has_side_effects=True, vmem_limit_bytes=48 << 20
        ),
    )(vectors, geo, transfer, jnp.asarray(direction_table(dir_count)), jnp.asarray(selectors()))
    lower_fac = jnp.linalg.cholesky(gram)
    ortho_basis = lax.linalg.triangular_solve(
        lower_fac, applied.astype(F32), left_side=True, lower=True
    )
    return (ortho_basis, lower_fac.T)


def solution(mesh):
    in_specs = (P(None, ("grp", "sub")), P(None, ("grp", "sub")), P(None, "grp", None, None))
    out_specs = (P(None, ("grp", "sub")), P())
    body = functools.partial(shards, mesh.shape["grp"], mesh.shape["sub"])
    return jax.shard_map(body, mesh=mesh, in_specs=in_specs, out_specs=out_specs, check_vma=False)
```

time: 767 us -> 119 us (0.16)
  the two profiles are of different devices: /device:TPU:24 before, /device:TPU:1 now
where the time goes in v1:
time: 119 us; the launch traced here: 118 us
  Pallas kernels  89.5 us (75%)
  other arithmetic  23.8 us (20%)
  local copies, waits for them, and re-layouts  2.77 us (2%)
  matrix products  1.59 us (1%)
    pallas_call x1, Pallas kernels, shards(): pl.pallas_call(functools.partial(product_kernel, n_grp, n_sub), out_shape...  89.5 us
    another operation x3, other arithmetic, shards(): lower_fac = jnp.linalg.cholesky(gram)  12.4 us
    another operation x1, other arithmetic, shards(): lax.linalg.triangular_solve(lower_fac, applied.astype(F32), left_side=Tru...  9.81 us
    unnamed x9, local copies, waits for them, and re-layouts  2.68 us

profile of v1, /device:TPU:1, one launch (start us, length us, event | category | flops | bytes accessed | tf_op | source)
XLA Modules:
  0.0 118.3 jit_solution(10399711509974929476)
XLA Ops:
  0.6 0.0 copy-start.3
  0.6 0.0 copy-start.2
  0.7 0.9 pad_maximum_fusion.geo
  1.6 0.0 copy-done.3
  1.6 0.0 copy-done.2
  1.6 0.0 copy-start
  1.6 1.0 copy-done
  2.6 0.0 copy-start.1
  2.6 0.9 copy-done.1
  3.5 89.5 %shard_map.68 = (bf16[128,2048]{1,0:T(8,128)(2,1)S(1)}, f32[128,128]{1,0:T(8,128)S(1)}) custom-call(bf16[128,2048]{1,0:T(8,128)(2,1)S(1)} %copy-done, bf16[16,2048]{1,0:T(8,128)(2,1)S(1)} %pad_maximum_fusion.geo, f32[2,1,4,512]{3,2,1,0:T(4,128)S(1)} %copy-done.2, bf16[512,16]{1,0:T(8,128)(2,1)S(1)} %copy-done.1, bf16[16,384]{1,0:T(8,128)(2,1)S(1)} %copy-done.3), custom_call_target="tpu_custom_call" | custom-call | tf_op jit(solution)/shard_map/pallas_call | solution.py:496
  93.0 0.1 copy.7
  93.1 11.7 %cholesky.16 = f32[128,128]{1,0:T(8,128)S(1)} custom-call(f32[128,128]{1,0:T(8,128)S(1)} %fusion.2), custom_call_target="Cholesky" | custom-call | tf_op jit(solution)/shard_map/jit(cholesky)/cholesky | solution.py:541
  104.9 0.6 compare_reduce_fusion
  105.5 0.7 fusion.3
  106.2 0.7 copy.8
  106.9 9.8 %custom-call.6 = f32[1,128,128]{1,2,0:T(8,128)S(1)} custom-call(f32[1,128,128]{2,1,0:T(8,128)S(1)} %get-tuple-element.9), custom_call_target="InvertDiagBlocksLowerTriangular" | custom-call | tf_op jit(solution)/shard_map/triangular_solve | solution.py:542
  116.7 1.6 %fusion = f32[128,2048]{1,0:T(8,128)} fusion(bf16[128,2048]{1,0:T(8,128)(2,1)S(1)} %get-tuple-element.5, f32[1,128,128]{1,2,0:T(8,128)S(1)} %custom-call.6), kind=kOutput, calls=%fused_computation.1 | convolution fusion | flops 402653184 | bytes 1638400 | tf_op jit(solution)/shard_map/triangular_solve | solution.py:542
  (2 shorter events, 0.0 us)
Async XLA Ops:
  0.6 0.9 copy-start.3
  0.6 0.9 copy-start.2
  1.6 1.0 copy-start
  2.6 0.9 copy-start.1

commit v2 on v1

--- a/solution.py
+++ b/solution.py
@@ -24,6 +24,7 @@
 
 TILE = 512
 ROWS = 64
+BLOCK = 16
 NT = (((1,), (1,)), ((), ()))
 TN = (((0,), (0,)), ((), ()))
 
@@ -61,14 +62,22 @@
 
 def product_kernel(
     n_grp, n_sub,
-    vec, geo, tran, dirs, sel,
+    vec_in, geo_in, tran_in, dirs_in,
     applied, gram,
-    wv, wv_nb, geo_nb, tables, moment, mom_recv, grp_src, grp_recv, tran_t, loc, loc_mat,
+    vec, geo_raw, tran, dirs, geo, wv, wv_nb, geo_nb, tables, moment, mom_recv, grp_src, grp_recv, tran_t, loc, loc_mat,
     xrep, yrep, w2, g, acc, q, z_send, z_recv,
     gram_src, gram_recv, gsum_recv, gram_all,
     halo_s, halo_r, mom_s, mom_r, grp_s, grp_r, loc_s, loc_r, z_s, z_r,
-    gr_s, gr_r, gg_s, gg_r, ga_s, ga_r,
+    gr_s, gr_r, gg_s, gg_r, ga_s, ga_r, in_s,
 ):
+    loads = [
+        pltpu.make_async_copy(src, dst, in_s.at[n])
+        for n, (src, dst) in enumerate(
+            ((geo_in, geo_raw), (vec_in, vec), (dirs_in, dirs), (tran_in, tran))
+        )
+    ]
+    for load in loads:
+        load.start()
     cols, panels = vec.shape
     dir_count = dirs.shape[0]
     chunk = dir_count // n_sub
@@ -98,6 +107,10 @@
 
     lax.fori_loop(1, n_grp, greet_g, 0)
 
+    for load in loads:
+        load.wait()
+    raw = geo_raw[...].astype(F32)
+    geo[...] = jnp.concatenate((raw,) * 4, 0).astype(BF16)
     weight = geo[3:4, :].astype(F32)
     wv[...] = (vec[...].astype(F32) * weight).astype(BF16)
 
@@ -162,10 +175,13 @@
 
     def source_side(geo_ref, wv_ref, base, offset):
         for k in range(3):
+            pick = lax.broadcasted_iota(jnp.int32, (16, 128), 0) == k
+            sel = jnp.where(pick, 1.0, 0.0).astype(BF16)
+
             def spread(n, _):
                 col = pl.multiple_of(n * TILE, TILE)
                 y = lax.dot_general(
-                    geo_ref[:, pl.ds(col, TILE)], sel[:, k * 128 : k * 128 + 128], TN,
+                    geo_ref[:, pl.ds(col, TILE)], sel, TN,
                     preferred_element_type=F32,
                 )
                 if k == 0 and offset:
@@ -464,6 +480,53 @@
     gram[...] = gram_all[...].reshape(cols, cols)
 
 
+def factor_kernel(gram, applied, ortho, upper, work, inverse):
+    n = gram.shape[0]
+    work[...] = gram[...]
+    sub = lax.broadcasted_iota(jnp.int32, (BLOCK, n), 0)
+    lane = lax.broadcasted_iota(jnp.int32, (BLOCK, n), 1)
+    for k in range(0, n, BLOCK):
+        rows = work[k : k + BLOCK, :]
+        col = [jnp.broadcast_to(rows[:, k + j : k + j + 1], (BLOCK, n)) for j in range(BLOCK)]
+        inside = (lane >= k) & (lane < k + BLOCK)
+        panel = jnp.where(inside, jnp.where(lane - k == sub, 1.0, 0.0), rows)
+        scale = jnp.ones((BLOCK, n), F32)
+        for j in range(BLOCK):
+            root = lax.rsqrt(jnp.broadcast_to(col[j][j : j + 1, :], (BLOCK, n)))
+            scale = jnp.where(sub == j, root, scale)
+            if j < BLOCK - 1:
+                ratio = jnp.where(sub > j, col[j] * (root * root), 0.0)
+                for l in range(j + 1, BLOCK):
+                    col[l] = col[l] - ratio * jnp.broadcast_to(col[l][j : j + 1, :], (BLOCK, n))
+                panel = panel - ratio * jnp.broadcast_to(panel[j : j + 1, :], (BLOCK, n))
+        panel = panel * scale
+        inverse[k : k + BLOCK, :] = jnp.where(lane < k + BLOCK, panel, 0.0)
+        corner = jnp.zeros((BLOCK, n), F32)
+        for j in range(BLOCK):
+            corner = jnp.where((lane == k + j) & (sub <= j), col[j], corner)
+        upper[k : k + BLOCK, :] = jnp.where(lane >= k + BLOCK, panel, corner * scale)
+        if k + BLOCK < n:
+            hi = panel.astype(BF16).astype(F32)
+            rest = panel - hi
+            mid = rest.astype(BF16).astype(F32)
+            lo = rest - mid
+            left = jnp.concatenate((hi, hi, mid, hi, lo, mid), 0).astype(BF16)
+            right = jnp.concatenate((hi, mid, hi, lo, hi, mid), 0).astype(BF16)
+            update = lax.dot_general(left, right, TN, preferred_element_type=F32)
+            below = work[k + BLOCK :, :]
+            at = lax.broadcasted_iota(jnp.int32, below.shape, 1)
+            below = jnp.where((at >= k) & (at < k + BLOCK), 0.0, below)
+            work[k + BLOCK :, :] = below - update[k + BLOCK :, :]
+    whole = inverse[...]
+    hi = whole.astype(BF16)
+    lo = (whole - hi.astype(F32)).astype(BF16)
+    for c in range(0, applied.shape[1], TILE):
+        tile = applied[:, c : c + TILE]
+        ortho[:, c : c + TILE] = jnp.dot(hi, tile, preferred_element_type=F32) + jnp.dot(
+            lo, tile, preferred_element_type=F32
+        )
+
+
 def direction_table(count):
     serial = np.arange(count).astype(np.float32)
     height = (1.0 - (2.0 * serial.astype(np.float64) + 1.0) / count)
@@ -478,20 +541,12 @@
     return table.astype(jnp.bfloat16)
 
 
-def selectors():
-    table = np.zeros((16, 3 * 128), np.float32)
-    for k in range(3):
-        table[k, k * 128 : k * 128 + 128] = 1.0
-    return table.astype(jnp.bfloat16)
-
-
 def shards(n_grp, n_sub, vectors, geometry, transfer):
     cols, panels = vectors.shape
     dir_count = transfer.shape[-1]
     chunk = dir_count // n_sub
     n_tiles = panels // TILE
     n_own = cols // 8
-    geo = jnp.concatenate((geometry,) * 4, 0)
     dma = pltpu.SemaphoreType.DMA
     applied, gram = pl.pallas_call(
         functools.partial(product_kernel, n_grp, n_sub),
@@ -499,9 +554,14 @@
             jax.ShapeDtypeStruct((cols, panels), BF16),
             jax.ShapeDtypeStruct((cols, cols), F32),
         ),
-        in_specs=[pl.BlockSpec(memory_space=pltpu.VMEM)] * 5,
+        in_specs=[pl.BlockSpec(memory_space=pl.ANY)] * 4,
         out_specs=[pl.BlockSpec(memory_space=pltpu.VMEM)] * 2,
         scratch_shapes=[
+            pltpu.VMEM((cols, panels), BF16),
+            pltpu.VMEM((4, panels), BF16),
+            pltpu.VMEM(transfer.shape, F32),
+            pltpu.VMEM((dir_count, 16), BF16),
+            pltpu.VMEM((16, panels), BF16),
             pltpu.VMEM((cols, panels), BF16),
             pltpu.VMEM((cols, panels), BF16),
             pltpu.VMEM((16, panels), BF16),
@@ -533,16 +593,25 @@
             dma((n_own,)), dma((n_sub,)),
             dma((n_grp,)), dma((n_grp,)),
             dma((n_sub,)), dma((n_own,)),
+            dma((4,)),
         ],
         compiler_params=pltpu.CompilerParams(
-            collective_id=0, has_side_effects=True, vmem_limit_bytes=48 << 20
+            collective_id=0, has_side_effects=True, vmem_limit_bytes=56 << 20
         ),
-    )(vectors, geo, transfer, jnp.asarray(direction_table(dir_count)), jnp.asarray(selectors()))
-    lower_fac = jnp.linalg.cholesky(gram)
-    ortho_basis = lax.linalg.triangular_solve(
-        lower_fac, applied.astype(F32), left_side=True, lower=True
+    )(vectors, geometry, transfer, jnp.asarray(direction_table(dir_count)))
+    return tuple(
+        pl.pallas_call(
+            factor_kernel,
+            out_shape=(
+                jax.ShapeDtypeStruct((cols, panels), F32),
+                jax.ShapeDtypeStruct((cols, cols), F32),
+            ),
+            in_specs=[pl.BlockSpec(memory_space=pltpu.VMEM)] * 2,
+            out_specs=[pl.BlockSpec(memory_space=pltpu.VMEM)] * 2,
+            scratch_shapes=[pltpu.VMEM((cols, cols), F32)] * 2,
+            compiler_params=pltpu.CompilerParams(vmem_limit_bytes=16 << 20),
+        )(gram, applied)
     )
-    return (ortho_basis, lower_fac.T)
 
 
 def solution(mesh):

time: 119 us -> 97.9 us (0.82)
  other arithmetic: 23.8 us -> 0 us
  Pallas kernels: 89.5 us -> 95.2 us
  matrix products: 1.59 us -> 0 us
    another operation x4 -> x0, other arithmetic: 22.2 us -> none  [the longest x3 12.4 us: shards(): lower_fac = jnp.linalg.cholesky(gram)]
    pallas_call x0 -> x1, Pallas kernels: none -> 4.93 us  [shards(): pl.pallas_call(factor_kernel, out_shape=(jax.ShapeDtypeStruct((cols, pane...]
    another operation x1 -> x0, matrix products: 1.59 us -> none  [shards(): lax.linalg.triangular_solve(lower_fac, applied.astype(F32), left_side=Tru...]
    unnamed x9 -> x4, local copies, waits for them, and re-layouts: 2.68 us -> 1.87 us
where the time goes in v2:
time: 97.9 us; the launch traced here: 97.7 us
  Pallas kernels  95.2 us (97%)
  local copies, waits for them, and re-layouts  1.87 us (2%)
    pallas_call x1, Pallas kernels, shards(): pl.pallas_call(functools.partial(product_kernel, n_grp, n_sub), out_shape...  90.3 us
    pallas_call x1, Pallas kernels, shards(): pl.pallas_call(factor_kernel, out_shape=(jax.ShapeDtypeStruct((cols, pane...  4.93 us

profile of v2, /device:TPU:1, one launch (start us, length us, event | category | flops | bytes accessed | tf_op | source)
XLA Modules:
  0.0 97.7 jit_solution(4544039149000281123)
XLA Ops:
  0.6 90.3 %shard_map.59 = (bf16[128,2048]{1,0:T(8,128)(2,1)}, f32[128,128]{1,0:T(8,128)}) custom-call(bf16[128,2048]{1,0:T(8,128)(2,1)} %vec_in.1, bf16[4,2048]{1,0:T(4,128)(2,1)} %geo_in.1, f32[2,1,4,512]{3,2,1,0:T(4,128)} %tran_in.1, bf16[512,16]{1,0:T(8,128)(2,1)} %constant.2.clone.dirs_in), custom_call_target="tpu_custom_call" | custom-call | tf_op jit(solution)/shard_map/pallas_call | solution.py:551
  90.9 0.0 copy-start
  90.9 1.0 %copy-done = bf16[128,2048]{1,0:T(8,128)(2,1)S(1)} copy-done((bf16[128,2048]{1,0:T(8,128)(2,1)S(1)}, bf16[128,2048]{1,0:T(8,128)(2,1)}, u32[]{:S(2)}) %copy-start) | copy-done | bytes 524312
  91.9 0.0 copy-start.1
  92.0 0.8 copy-done.1
  92.8 4.9 %shard_map.60 = (f32[128,2048]{1,0:T(8,128)}, f32[128,128]{1,0:T(8,128)}) custom-call(f32[128,128]{1,0:T(8,128)S(1)} %copy-done.1, bf16[128,2048]{1,0:T(8,128)(2,1)S(1)} %copy-done), custom_call_target="tpu_custom_call" | custom-call | tf_op jit(solution)/shard_map/pallas_call | solution.py:603
Async XLA Ops:
  90.9 1.0 %copy-start = (bf16[128,2048]{1,0:T(8,128)(2,1)S(1)}, bf16[128,2048]{1,0:T(8,128)(2,1)}, u32[]{:S(2)}) copy-start(bf16[128,2048]{1,0:T(8,128)(2,1)} %get-tuple-element.5.applied) | copy-start | bytes 1572868
  91.9 0.8 copy-start.1

commit v3 on v2

--- a/solution.py
+++ b/solution.py
@@ -65,7 +65,7 @@
     vec_in, geo_in, tran_in, dirs_in,
     applied, gram,
     vec, geo_raw, tran, dirs, geo, wv, wv_nb, geo_nb, tables, moment, mom_recv, grp_src, grp_recv, tran_t, loc, loc_mat,
-    xrep, yrep, w2, g, acc, q, z_send, z_recv,
+    xrep, yrep, g, acc, z_acc, z_send, z_recv,
     gram_src, gram_recv, gsum_recv, gram_all,
     halo_s, halo_r, mom_s, mom_r, grp_s, grp_r, loc_s, loc_r, z_s, z_r,
     gr_s, gr_r, gg_s, gg_r, ga_s, ga_r, in_s,
@@ -114,8 +114,6 @@
     weight = geo[3:4, :].astype(F32)
     wv[...] = (vec[...].astype(F32) * weight).astype(BF16)
 
-    pl.semaphore_wait(barrier, n_sub - 1 + n_grp - 1)
-
     def halo(dst_sub):
         return (
             remote(wv, wv_nb, halo_s.at[0], halo_r.at[0], {"sub": dst_sub}),
@@ -125,17 +123,14 @@
     left = lax.rem(me_s + n_sub - 1, n_sub)
     right = lax.rem(me_s + 1, n_sub)
 
-    @pl.when(has_left)
-    def _():
-        for copy in halo(left):
-            copy.start()
+    half = panels // 2
 
     def far_tables(n, _):
-        k = n // n_tiles
-        col = pl.multiple_of((n % n_tiles) * TILE, TILE)
+        k = n // 2
+        col = pl.multiple_of((n % 2) * half, half)
         turns = jnp.dot(
             dirs[pl.ds(pl.multiple_of(k * 128, 128), 128), :],
-            geo[:, pl.ds(col, TILE)],
+            geo[:, pl.ds(col, half)],
             preferred_element_type=F32,
         )
         a, b = half_angle(turns)
@@ -143,11 +138,18 @@
         norm = aa + bb
         inv = lax.rsqrt(norm * norm)
         row = pl.multiple_of(k * 256, 256)
-        tables[pl.ds(row, 128), pl.ds(col, TILE)] = ((aa - bb) * inv).astype(BF16)
-        tables[pl.ds(row + 128, 128), pl.ds(col, TILE)] = (a * b * inv).astype(BF16)
-        return 0
-
-    lax.fori_loop(0, dir_count // 128 * n_tiles, far_tables, 0)
+        tables[pl.ds(row, 128), pl.ds(col, half)] = ((aa - bb) * inv).astype(BF16)
+        tables[pl.ds(row + 128, 128), pl.ds(col, half)] = (a * b * inv).astype(BF16)
+        return 0
+
+    lax.fori_loop(0, dir_count // 128 * 2, far_tables, 0)
+
+    pl.semaphore_wait(barrier, n_sub - 1 + n_grp - 1)
+
+    @pl.when(has_left)
+    def _():
+        for copy in halo(left):
+            copy.start()
 
     moment_scale = (panels * n_sub) ** (-0.5)
     for k in range(dir_count // 128):
@@ -173,32 +175,26 @@
     for k in range(3):
         xrep[k] = jnp.broadcast_to(geo[k : k + 1, :].astype(F32) * TURN, (8, panels))
 
-    def source_side(geo_ref, wv_ref, base, offset):
-        for k in range(3):
-            pick = lax.broadcasted_iota(jnp.int32, (16, 128), 0) == k
-            sel = jnp.where(pick, 1.0, 0.0).astype(BF16)
-
-            def spread(n, _):
-                col = pl.multiple_of(n * TILE, TILE)
-                y = lax.dot_general(
-                    geo_ref[:, pl.ds(col, TILE)], sel, TN,
-                    preferred_element_type=F32,
-                )
+    def source_side(geo_ref, base, offset):
+        rows = lax.broadcasted_iota(jnp.int32, (16, 3 * 128), 0)
+        lanes = lax.broadcasted_iota(jnp.int32, (16, 3 * 128), 1)
+        pick = (lanes >= rows * 128) & (lanes < rows * 128 + 128)
+        sel = jnp.where(pick, 1.0, 0.0).astype(BF16)
+
+        for col in range(0, panels, TILE):
+            y = lax.dot_general(
+                geo_ref[:, col : col + TILE], sel, TN, preferred_element_type=F32
+            )
+            for k in range(3):
+                part = y[:, k * 128 : k * 128 + 128]
                 if k == 0 and offset:
-                    y = y + float(offset)
-                yrep[k, pl.ds(base + col, TILE), :] = y * TURN
-                return 0
-            lax.fori_loop(0, n_tiles, spread, 0)
-        for n in range(panels // 128):
-            block = wv_ref[:, n * 128 : n * 128 + 128].astype(F32)
-            at = 2 * base + n * 256
-            w2[:, at : at + 128] = block.astype(BF16)
-            w2[:, at + 128 : at + 256] = (2.0 * rotated(block, 0)).astype(BF16)
-
-    source_side(geo, wv, 0, 0)
+                    part = part + float(offset)
+                yrep[k, base + col : base + col + TILE, :] = part * TURN
+
+    source_side(geo, 0, 0)
     acc[...] = jnp.zeros_like(acc)
 
-    def near_tile(source, target, symmetric):
+    def near_tile(source, target, weighted, mirror):
         i0 = pl.multiple_of(target * TILE, TILE)
 
         def strip(r, _):
@@ -217,69 +213,64 @@
                     aa, bb = a * a, b * b
                     norm = aa + bb
                     inv = lax.rsqrt(norm * norm * (d2 + SOFT))
-                    at = pl.multiple_of(
-                        (r * ROWS) // 128 * 256 + lax.rem(r * ROWS, 128), ROWS
-                    ) + sub
+                    at = pl.multiple_of(r * ROWS, ROWS) + sub
                     g[pl.ds(at, 16), l : l + 128] = (
                         ((aa - bb) * inv).reshape(16, 128).astype(BF16)
                     )
-                    g[pl.ds(at + 128, 16), l : l + 128] = (
+                    g[pl.ds(at + TILE, 16), l : l + 128] = (
                         ((a * b) * inv).reshape(16, 128).astype(BF16)
                     )
             return 0
 
         lax.fori_loop(0, TILE // ROWS, strip, 0)
-        acc[:, pl.ds(i0, TILE)] += jnp.dot(
-            w2[:, pl.ds(pl.multiple_of(source * 2 * TILE, 2 * TILE), 2 * TILE)],
-            g[...],
-            preferred_element_type=F32,
-        )
-        if symmetric:
-            q[...] += lax.dot_general(
-                wv[:, pl.ds(i0, TILE)], g[...], NT, preferred_element_type=F32
+        for part in range(2):
+            acc[part * cols : part * cols + cols, pl.ds(i0, TILE)] += jnp.dot(
+                weighted, g[part * TILE : part * TILE + TILE, :], preferred_element_type=F32
             )
-
-    def mirrored(n):
-        re = q[:, n * 256 : n * 256 + 128]
-        im = q[:, n * 256 + 128 : n * 256 + 256]
+        if mirror is not None:
+            ref, at = mirror
+            for part in range(2):
+                ref[part * cols : part * cols + cols, at : at + TILE] += lax.dot_general(
+                    wv[:, pl.ds(i0, TILE)], g[part * TILE : part * TILE + TILE, :], NT,
+                    preferred_element_type=F32,
+                )
+
+    def joined(re, im):
         return re + 2.0 * rotated(im, 0)
 
     def send_z(j):
         return remote(z_send.at[j], z_recv.at[j], z_s.at[j], z_r.at[j], {"sub": right})
 
-    @pl.when(has_right)
-    def _():
-        for copy in halo(left):
-            copy.wait_recv()
-        source_side(geo_nb, wv_nb, panels, 1)
+    def neighbour_start():
+        @pl.when(has_right)
+        def _():
+            for copy in halo(left):
+                copy.wait_recv()
+            source_side(geo_nb, panels, 1)
 
     def neighbour_block(j):
         @pl.when(has_right)
         def _():
-            q[...] = jnp.zeros_like(q)
+            z_acc[...] = jnp.zeros_like(z_acc)
 
             def step(i, _):
-                near_tile(n_tiles + j, i, True)
+                near_tile(n_tiles + j, i, wv_nb[:, j * TILE : j * TILE + TILE], (z_acc, 0))
                 return 0
 
             lax.fori_loop(0, n_tiles, step, 0)
-            for n in range(TILE // 128):
-                z_send[j, :, n * 128 : n * 128 + 128] = mirrored(n).astype(BF16)
+            z_send[j] = joined(z_acc[:cols], z_acc[cols:]).astype(BF16)
             send_z(j).start()
 
     def own_block(j):
-        near_tile(j, j, False)
+        weighted = wv[:, j * TILE : j * TILE + TILE]
+        near_tile(j, j, weighted, None)
         if j < n_tiles - 1:
-            q[...] = jnp.zeros_like(q)
 
             def step(i, _):
-                near_tile(j, i, True)
+                near_tile(j, i, weighted, (acc, j * TILE))
                 return 0
 
             lax.fori_loop(j + 1, n_tiles, step, 0)
-            for n in range(TILE // 128):
-                at = j * TILE + n * 128
-                acc[:, at : at + 128] += mirrored(n)
 
     def reduce_moment():
         def arrived(k, _):
@@ -328,13 +319,15 @@
 
         lax.fori_loop(1, n_sub, send, 0)
 
+    own_block(0)
+    neighbour_start()
     neighbour_block(0)
     reduce_moment()
     neighbour_block(1)
     translate()
     for j in range(2, n_tiles):
         neighbour_block(j)
-    for j in range(n_tiles):
+    for j in range(1, n_tiles):
         own_block(j)
 
     def loc_arrived(k, _):
@@ -355,7 +348,7 @@
             copy.wait_send()
         for j in range(n_tiles):
             send_z(j).wait_recv()
-            acc[:, j * TILE : j * TILE + TILE] += z_recv[j].astype(F32)
+            acc[:cols, j * TILE : j * TILE + TILE] += z_recv[j].astype(F32)
 
     @pl.when(has_right)
     def _():
@@ -369,7 +362,7 @@
         at = slice(j * TILE, j * TILE + TILE)
         far = jnp.dot(loc_mat[...], tables[:, at], preferred_element_type=F32)
         tile = (
-            0.5 * vec[:, at].astype(F32) + near_scale * acc[:, at] + far_scale * far
+            0.5 * vec[:, at].astype(F32) + near_scale * joined(acc[:cols, at], acc[cols:, at]) + far_scale * far
         ).astype(BF16)
         applied[:, at] = tile
         partial = partial + lax.dot_general(tile, tile, NT, preferred_element_type=F32)
@@ -480,9 +473,13 @@
     gram[...] = gram_all[...].reshape(cols, cols)
 
 
-def factor_kernel(gram, applied, ortho, upper, work, inverse):
+def factor_kernel(gram, applied_in, ortho, upper, work, inverse, applied, sems):
     n = gram.shape[0]
-    work[...] = gram[...]
+    load_gram = pltpu.make_async_copy(gram, work, sems.at[0])
+    load_applied = pltpu.make_async_copy(applied_in, applied, sems.at[1])
+    load_gram.start()
+    load_applied.start()
+    load_gram.wait()
     sub = lax.broadcasted_iota(jnp.int32, (BLOCK, n), 0)
     lane = lax.broadcasted_iota(jnp.int32, (BLOCK, n), 1)
     for k in range(0, n, BLOCK):
@@ -517,6 +514,7 @@
             at = lax.broadcasted_iota(jnp.int32, below.shape, 1)
             below = jnp.where((at >= k) & (at < k + BLOCK), 0.0, below)
             work[k + BLOCK :, :] = below - update[k + BLOCK :, :]
+    load_applied.wait()
     whole = inverse[...]
     hi = whole.astype(BF16)
     lo = (whole - hi.astype(F32)).astype(BF16)
@@ -575,10 +573,9 @@
             pltpu.VMEM((cols, 2 * dir_count), BF16),
             pltpu.VMEM((3, 8, panels), F32),
             pltpu.VMEM((3, 2 * panels, 128), F32),
-            pltpu.VMEM((cols, 4 * panels), BF16),
             pltpu.VMEM((2 * TILE, TILE), BF16),
-            pltpu.VMEM((cols, panels), F32),
-            pltpu.VMEM((cols, 2 * TILE), F32),
+            pltpu.VMEM((2 * cols, panels), F32),
+            pltpu.VMEM((2 * cols, TILE), F32),
             pltpu.VMEM((n_tiles, cols, TILE), BF16),
             pltpu.VMEM((n_tiles, cols, TILE), BF16),
             pltpu.VMEM((n_own, 8, cols), F32),
@@ -606,10 +603,15 @@
                 jax.ShapeDtypeStruct((cols, panels), F32),
                 jax.ShapeDtypeStruct((cols, cols), F32),
             ),
-            in_specs=[pl.BlockSpec(memory_space=pltpu.VMEM)] * 2,
+            in_specs=[pl.BlockSpec(memory_space=pl.ANY)] * 2,
             out_specs=[pl.BlockSpec(memory_space=pltpu.VMEM)] * 2,
-            scratch_shapes=[pltpu.VMEM((cols, cols), F32)] * 2,
-            compiler_params=pltpu.CompilerParams(vmem_limit_bytes=16 << 20),
+            scratch_shapes=[
+                pltpu.VMEM((cols, cols), F32),
+                pltpu.VMEM((cols, cols), F32),
+                pltpu.VMEM((cols, panels), BF16),
+                dma((2,)),
+            ],
+            compiler_params=pltpu.CompilerParams(vmem_limit_bytes=56 << 20),
         )(gram, applied)
     )
 

time: 97.9 us -> 89 us (0.909)
  Pallas kernels: 95.2 us -> 88 us
  local copies, waits for them, and re-layouts: 1.87 us -> 0 us
    pallas_call x1, Pallas kernels: 90.3 us -> 82.2 us  [shards(): pl.pallas_call(functools.partial(product_kernel, n_grp, n_sub), out_shape...]
    unnamed x4 -> x0, local copies, waits for them, and re-layouts: 1.87 us -> none
where the time goes in v3:
time: 89 us; the launch traced here: 88.8 us
  Pallas kernels  88 us (99%)
    pallas_call x1, Pallas kernels, shards(): pl.pallas_call(functools.partial(product_kernel, n_grp, n_sub), out_shape...  82.2 us
    pallas_call x1, Pallas kernels, shards(): pl.pallas_call(factor_kernel, out_shape=(jax.ShapeDtypeStruct((cols, pane...  5.83 us

profile of v3, /device:TPU:1, one launch (start us, length us, event | category | flops | bytes accessed | tf_op | source)
XLA Modules:
  0.0 88.8 jit_solution(620923149272690139)
XLA Ops:
  0.6 82.2 %shard_map.59 = (bf16[128,2048]{1,0:T(8,128)(2,1)}, f32[128,128]{1,0:T(8,128)}) custom-call(bf16[128,2048]{1,0:T(8,128)(2,1)} %vec_in.1, bf16[4,2048]{1,0:T(4,128)(2,1)} %geo_in.1, f32[2,1,4,512]{3,2,1,0:T(4,128)} %tran_in.1, bf16[512,16]{1,0:T(8,128)(2,1)} %constant.2.clone.dirs_in), custom_call_target="tpu_custom_call" | custom-call | tf_op jit(solution)/shard_map/pallas_call | solution.py:549
  82.8 5.8 %shard_map.60 = (f32[128,2048]{1,0:T(8,128)}, f32[128,128]{1,0:T(8,128)}) custom-call(f32[128,128]{1,0:T(8,128)} %get-tuple-element.4.gram, bf16[128,2048]{1,0:T(8,128)(2,1)} %get-tuple-element.5.applied_in), custom_call_target="tpu_custom_call" | custom-call | tf_op jit(solution)/shard_map/pallas_call | solution.py:600

commit v4 on v3

--- a/solution.py
+++ b/solution.py
@@ -20,7 +20,6 @@
 SOFT = DELTA * DELTA * TURN * TURN
 Q0 = -1.03910273
 P0, P1, P2 = -0.33076115, 1.40669993, -0.3346358
-MAGIC = 1.5 * 2.0**23
 
 TILE = 512
 ROWS = 64
@@ -30,7 +29,7 @@
 
 
 def half_angle(t):
-    f = t - ((t + MAGIC) - MAGIC)
+    f = t - jnp.round(t)
     u = f * f
     return (P2 * u + P1) * u + P0, f * (u + Q0)
 
@@ -73,7 +72,7 @@
     loads = [
         pltpu.make_async_copy(src, dst, in_s.at[n])
         for n, (src, dst) in enumerate(
-            ((geo_in, geo_raw), (vec_in, vec), (dirs_in, dirs), (tran_in, tran))
+            ((geo_in, geo_raw), (dirs_in, dirs), (vec_in, vec), (tran_in, tran))
         )
     ]
     for load in loads:
@@ -107,12 +106,10 @@
 
     lax.fori_loop(1, n_grp, greet_g, 0)
 
-    for load in loads:
+    for load in loads[:2]:
         load.wait()
     raw = geo_raw[...].astype(F32)
     geo[...] = jnp.concatenate((raw,) * 4, 0).astype(BF16)
-    weight = geo[3:4, :].astype(F32)
-    wv[...] = (vec[...].astype(F32) * weight).astype(BF16)
 
     def halo(dst_sub):
         return (
@@ -144,6 +141,11 @@
 
     lax.fori_loop(0, dir_count // 128 * 2, far_tables, 0)
 
+    for load in loads[2:]:
+        load.wait()
+    weight = geo[3:4, :].astype(F32)
+    wv[...] = (vec[...].astype(F32) * weight).astype(BF16)
+
     pl.semaphore_wait(barrier, n_sub - 1 + n_grp - 1)
 
     @pl.when(has_left)
@@ -166,7 +168,7 @@
     def send_moment(k, _):
         p = peer(k)
         remote(
-            rows_of(moment, p, chunk), mom_recv.at[me_s], mom_s.at[p], mom_r.at[me_s], {"sub": p}
+            rows_of(moment, p, chunk), mom_recv.at[me_s], mom_s.at[0], mom_r.at[0], {"sub": p}
         ).start()
         return 0
 
@@ -273,15 +275,9 @@
             lax.fori_loop(j + 1, n_tiles, step, 0)
 
     def reduce_moment():
-        def arrived(k, _):
-            p = peer(k)
-            remote(
-                rows_of(moment, p, chunk), mom_recv.at[p], mom_s.at[p], mom_r.at[p], {"sub": p}
-            ).wait()
-            return 0
-
+        rest = mom_recv.at[pl.ds(0, n_sub - 1)]
+        remote(rest, rest, mom_s.at[0], mom_r.at[0], {"sub": right}).wait()
         mom_recv[me_s] = moment[pl.ds(pl.multiple_of(me_s * chunk, chunk), chunk), :]
-        lax.fori_loop(1, n_sub, arrived, 0)
         total = mom_recv[0]
         for n in range(1, n_sub):
             total = total + mom_recv[n]
@@ -314,12 +310,13 @@
 
         def send(k, _):
             p = peer(k)
-            remote(loc.at[me_s], loc.at[me_s], loc_s.at[p], loc_r.at[me_s], {"sub": p}).start()
+            remote(loc.at[me_s], loc.at[me_s], loc_s.at[0], loc_r.at[0], {"sub": p}).start()
             return 0
 
         lax.fori_loop(1, n_sub, send, 0)
 
     own_block(0)
+    own_block(1)
     neighbour_start()
     neighbour_block(0)
     reduce_moment()
@@ -327,15 +324,11 @@
     translate()
     for j in range(2, n_tiles):
         neighbour_block(j)
-    for j in range(1, n_tiles):
+    for j in range(2, n_tiles):
         own_block(j)
 
-    def loc_arrived(k, _):
-        p = peer(k)
-        remote(loc.at[me_s], loc.at[p], loc_s.at[p], loc_r.at[p], {"sub": p}).wait()
-        return 0
-
-    lax.fori_loop(1, n_sub, loc_arrived, 0)
+    rest = loc.at[pl.ds(0, n_sub - 1)]
+    remote(rest, rest, loc_s.at[0], loc_r.at[0], {"sub": right}).wait()
     per = 128 // chunk
     for k in range(dir_count // 128):
         block = jnp.concatenate([loc[k * per + n].astype(F32) for n in range(per)], 0)
@@ -374,103 +367,77 @@
     owner = lax.rem(me_s, stride) == 0
     gram_src[...] = partial.reshape(n_own, 8, cols)
 
-    def gram_copy(c, slot, sem):
-        return remote(
-            gram_src.at[c], gram_recv.at[slot], gr_s.at[c], gr_r.at[sem], {"sub": c * stride}
-        )
+    def send_block(c):
+        remote(
+            gram_src.at[c], gram_recv.at[me_s], gr_s.at[0], gr_r.at[0], {"sub": c * stride}
+        ).start()
+
+    def wait_for(ref, count, send_sem, recv_sem):
+        part = ref.at[pl.ds(0, count)]
+        return remote(part, part, send_sem.at[0], recv_sem.at[0], {"sub": right})
 
     def send_gram(k, _):
-        c = lax.rem(mine + k, n_own)
-        gram_copy(c, me_s, me_s).start()
+        send_block(lax.rem(mine + k, n_own))
         return 0
 
     lax.fori_loop(1, n_own, send_gram, 0)
 
     @pl.when(jnp.logical_not(owner))
     def _():
-        gram_copy(mine, me_s, me_s).start()
+        send_block(mine)
 
     @pl.when(owner)
     def _():
+        wait_for(gram_recv, n_sub - 1, gr_s, gr_r).wait_recv()
         gram_recv[me_s] = gram_src[mine]
-
-        def arrived(k, _):
-            p = peer(k)
-            gram_copy(mine, p, p).wait_recv()
-            return 0
-
-        lax.fori_loop(1, n_sub, arrived, 0)
         total = gram_recv[0]
         for n in range(1, n_sub):
             total = total + gram_recv[n]
         gsum_recv[me_g] = total
 
-        def swap(k, _):
+        def swap(k):
             p = peer_g(k)
-            remote(
+            return remote(
                 gsum_recv.at[me_g], gsum_recv.at[me_g], gg_s.at[p], gg_r.at[me_g], {"grp": p}
-            ).start()
-            return 0
-
-        lax.fori_loop(1, n_grp, swap, 0)
-
-        def swapped(k, _):
+            )
+
+        def swapped(k):
             p = peer_g(k)
-            remote(
+            return remote(
                 gsum_recv.at[me_g], gsum_recv.at[p], gg_s.at[p], gg_r.at[p], {"grp": p}
-            ).wait()
-            return 0
-
-        lax.fori_loop(1, n_grp, swapped, 0)
+            )
+
+        for k in range(1, n_grp):
+            swap(k).start()
+        for k in range(1, n_grp):
+            swapped(k).wait_recv()
         total = gsum_recv[0]
         for n in range(1, n_grp):
             total = total + gsum_recv[n]
         gram_all[mine] = total
 
         def spread(k, _):
-            p = peer(k)
             remote(
-                gram_all.at[mine], gram_all.at[mine], ga_s.at[p], ga_r.at[mine], {"sub": p}
+                gram_all.at[mine], gram_all.at[mine], ga_s.at[0], ga_r.at[0], {"sub": peer(k)}
             ).start()
             return 0
 
         lax.fori_loop(1, n_sub, spread, 0)
-
-    def gathered(k, _):
-        c = lax.rem(mine + k, n_own)
-        remote(
-            gram_all.at[c], gram_all.at[c], ga_s.at[c], ga_r.at[c], {"sub": c * stride}
-        ).wait_recv()
-        return 0
-
-    lax.fori_loop(1, n_own, gathered, 0)
+        for k in range(1, n_grp):
+            swap(k).wait_send()
+        wait_for(gram_src, n_own - 1, gr_s, gr_r).wait_send()
+        wait_for(gram_all, n_own - 1, ga_s, ga_r).wait_recv()
 
     @pl.when(jnp.logical_not(owner))
     def _():
-        remote(
-            gram_all.at[mine], gram_all.at[mine], ga_s.at[mine], ga_r.at[mine],
-            {"sub": mine * stride},
-        ).wait_recv()
-        gram_copy(mine, me_s, me_s).wait_send()
-
-    def sent(k, _):
-        gram_copy(lax.rem(mine + k, n_own), me_s, me_s).wait_send()
-        return 0
-
-    lax.fori_loop(1, n_own, sent, 0)
+        wait_for(gram_src, n_own, gr_s, gr_r).wait_send()
+        wait_for(gram_all, n_own, ga_s, ga_r).wait_recv()
+
+    gram[...] = gram_all[...].reshape(cols, cols)
 
     @pl.when(owner)
     def _():
-        def spread_sent(k, _):
-            p = peer(k)
-            remote(
-                gram_all.at[mine], gram_all.at[mine], ga_s.at[p], ga_r.at[mine], {"sub": p}
-            ).wait_send()
-            return 0
-
-        lax.fori_loop(1, n_sub, spread_sent, 0)
-
-    gram[...] = gram_all[...].reshape(cols, cols)
+        wait_for(gram_recv, n_sub - 1, ga_s, ga_r).wait_send()
 
 
 def factor_kernel(gram, applied_in, ortho, upper, work, inverse, applied, sems):
@@ -583,13 +550,13 @@
             pltpu.VMEM((n_grp, 8, cols), F32),
             pltpu.VMEM((n_own, 8, cols), F32),
             dma((2,)), dma((2,)),
-            dma((n_sub,)), dma((n_sub,)),
+            dma((1,)), dma((1,)),
             dma((n_grp,)), dma((n_grp,)),
-            dma((n_sub,)), dma((n_sub,)),
+            dma((1,)), dma((1,)),
             dma((n_tiles,)), dma((n_tiles,)),
-            dma((n_own,)), dma((n_sub,)),
+            dma((1,)), dma((1,)),
             dma((n_grp,)), dma((n_grp,)),
-            dma((n_sub,)), dma((n_own,)),
+            dma((1,)), dma((1,)),
             dma((4,)),
         ],
         compiler_params=pltpu.CompilerParams(

time: 89 us -> 84 us (0.944)
  Pallas kernels: 88 us -> 83.2 us
    pallas_call x1, Pallas kernels: 82.2 us -> 77.4 us  [shards(): pl.pallas_call(functools.partial(product_kernel, n_grp, n_sub), out_shape...]
where the time goes in v4:
time: 84 us; the launch traced here: 83.9 us
  Pallas kernels  83.2 us (99%)
    pallas_call x1, Pallas kernels, shards(): pl.pallas_call(functools.partial(product_kernel, n_grp, n_sub), out_shape...  77.4 us
    pallas_call x1, Pallas kernels, shards(): pl.pallas_call(factor_kernel, out_shape=(jax.ShapeDtypeStruct((cols, pane...  5.83 us

profile of v4, /device:TPU:1, one launch (start us, length us, event | category | flops | bytes accessed | tf_op | source)
XLA Modules:
  0.0 83.9 jit_solution(7174487083025909168)
XLA Ops:
  0.6 77.4 %shard_map.59 = (bf16[128,2048]{1,0:T(8,128)(2,1)}, f32[128,128]{1,0:T(8,128)}) custom-call(bf16[128,2048]{1,0:T(8,128)(2,1)} %vec_in.1, bf16[4,2048]{1,0:T(4,128)(2,1)} %geo_in.1, f32[2,1,4,512]{3,2,1,0:T(4,128)} %tran_in.1, bf16[512,16]{1,0:T(8,128)(2,1)} %constant.2.clone.dirs_in), custom_call_target="tpu_custom_call" | custom-call | tf_op jit(solution)/shard_map/pallas_call | solution.py:516
  78.0 5.8 %shard_map.60 = (f32[128,2048]{1,0:T(8,128)}, f32[128,128]{1,0:T(8,128)}) custom-call(f32[128,128]{1,0:T(8,128)} %get-tuple-element.4.gram, bf16[128,2048]{1,0:T(8,128)(2,1)} %get-tuple-element.5.applied_in), custom_call_target="tpu_custom_call" | custom-call | tf_op jit(solution)/shard_map/pallas_call | solution.py:567

commit v5 on v4

--- a/solution.py
+++ b/solution.py
@@ -62,12 +62,12 @@
 def product_kernel(
     n_grp, n_sub,
     vec_in, geo_in, tran_in, dirs_in,
-    applied, gram,
+    applied_out, gram,
     vec, geo_raw, tran, dirs, geo, wv, wv_nb, geo_nb, tables, moment, mom_recv, grp_src, grp_recv, tran_t, loc, loc_mat,
     xrep, yrep, g, acc, z_acc, z_send, z_recv,
     gram_src, gram_recv, gsum_recv, gram_all,
     halo_s, halo_r, mom_s, mom_r, grp_s, grp_r, loc_s, loc_r, z_s, z_r,
-    gr_s, gr_r, gg_s, gg_r, ga_s, ga_r, in_s,
+    gr_s, gr_r, gg_s, gg_r, ga_s, ga_r, in_s, applied, out_s,
 ):
     loads = [
         pltpu.make_async_copy(src, dst, in_s.at[n])
@@ -165,14 +165,12 @@
     def rows_of(ref, i, size):
         return ref.at[pl.ds(pl.multiple_of(i * size, size), size), :]
 
-    def send_moment(k, _):
+    def send_moment(k):
         p = peer(k)
         remote(
             rows_of(moment, p, chunk), mom_recv.at[me_s], mom_s.at[0], mom_r.at[0], {"sub": p}
         ).start()
-        return 0
-
-    lax.fori_loop(1, n_sub, send_moment, 0)
+
 
     for k in range(3):
         xrep[k] = jnp.broadcast_to(geo[k : k + 1, :].astype(F32) * TURN, (8, panels))
@@ -196,11 +194,18 @@
     source_side(geo, 0, 0)
     acc[...] = jnp.zeros_like(acc)
 
-    def near_tile(source, target, weighted, mirror):
+    def near_tile(source, target, weighted, mirror, send=None):
         i0 = pl.multiple_of(target * TILE, TILE)
 
-        def strip(r, _):
-            for l in range(0, TILE, 128):
+        def strip(first, r, _):
+            if send is not None:
+                k = target * (TILE // ROWS) + r
+
+                @pl.when(k > 0)
+                def _():
+                    send(k)
+
+            for l in range(first, TILE, 128):
                 for sub in range(0, ROWS, 16):
                     row = pl.multiple_of(source * TILE + r * ROWS, ROWS) + sub
 
@@ -224,18 +229,36 @@
                     )
             return 0
 
-        lax.fori_loop(0, TILE // ROWS, strip, 0)
+        strips = TILE // ROWS
+        if mirror is None:
+            half = TILE // 2
+            lax.fori_loop(0, strips // 2, functools.partial(strip, 0), 0)
+            lax.fori_loop(strips // 2, strips, functools.partial(strip, half), 0)
+            for part in range(2):
+                at = slice(part * cols, part * cols + cols)
+                upper = slice(part * TILE, part * TILE + half)
+                near, far = pl.ds(i0, half), pl.ds(i0 + half, half)
+                acc[at, near] += jnp.dot(
+                    weighted[:, :half], g[upper, :half], preferred_element_type=F32
+                ) + lax.dot_general(
+                    wv[:, far], g[upper, half:], NT, preferred_element_type=F32
+                )
+                acc[at, far] += jnp.dot(
+                    weighted, g[part * TILE : part * TILE + TILE, half:],
+                    preferred_element_type=F32,
+                )
+            return
+        lax.fori_loop(0, strips, functools.partial(strip, 0), 0)
         for part in range(2):
             acc[part * cols : part * cols + cols, pl.ds(i0, TILE)] += jnp.dot(
                 weighted, g[part * TILE : part * TILE + TILE, :], preferred_element_type=F32
             )
-        if mirror is not None:
-            ref, at = mirror
-            for part in range(2):
-                ref[part * cols : part * cols + cols, at : at + TILE] += lax.dot_general(
-                    wv[:, pl.ds(i0, TILE)], g[part * TILE : part * TILE + TILE, :], NT,
-                    preferred_element_type=F32,
-                )
+        ref, at = mirror
+        for part in range(2):
+            ref[part * cols : part * cols + cols, at : at + TILE] += lax.dot_general(
+                wv[:, pl.ds(i0, TILE)], g[part * TILE : part * TILE + TILE, :], NT,
+                preferred_element_type=F32,
+            )
 
     def joined(re, im):
         return re + 2.0 * rotated(im, 0)
@@ -250,26 +273,28 @@
                 copy.wait_recv()
             source_side(geo_nb, panels, 1)
 
-    def neighbour_block(j):
+    def neighbour_block(j, send=None):
         @pl.when(has_right)
         def _():
             z_acc[...] = jnp.zeros_like(z_acc)
 
             def step(i, _):
-                near_tile(n_tiles + j, i, wv_nb[:, j * TILE : j * TILE + TILE], (z_acc, 0))
+                near_tile(
+                    n_tiles + j, i, wv_nb[:, j * TILE : j * TILE + TILE], (z_acc, 0), send
+                )
                 return 0
 
             lax.fori_loop(0, n_tiles, step, 0)
             z_send[j] = joined(z_acc[:cols], z_acc[cols:]).astype(BF16)
             send_z(j).start()
 
-    def own_block(j):
+    def own_block(j, send=None):
         weighted = wv[:, j * TILE : j * TILE + TILE]
-        near_tile(j, j, weighted, None)
+        near_tile(j, j, weighted, None, send)
         if j < n_tiles - 1:
 
             def step(i, _):
-                near_tile(j, i, weighted, (acc, j * TILE))
+                near_tile(j, i, weighted, (acc, j * TILE), send)
                 return 0
 
             lax.fori_loop(j + 1, n_tiles, step, 0)
@@ -308,21 +333,28 @@
             total = total + coef[:, n_grp + h : n_grp + h + 1] * lane_rotated(m)
         loc[me_s] = total.astype(BF16)
 
-        def send(k, _):
-            p = peer(k)
-            remote(loc.at[me_s], loc.at[me_s], loc_s.at[0], loc_r.at[0], {"sub": p}).start()
-            return 0
-
-        lax.fori_loop(1, n_sub, send, 0)
-
-    own_block(0)
+    def send_local(k):
+        remote(loc.at[me_s], loc.at[me_s], loc_s.at[0], loc_r.at[0], {"sub": peer(k)}).start()
+
+    assert n_tiles * (TILE // ROWS) == n_sub
+    own_block(0, send_moment)
     own_block(1)
     neighbour_start()
     neighbour_block(0)
     reduce_moment()
     neighbour_block(1)
     translate()
-    for j in range(2, n_tiles):
+
+    @pl.when(jnp.logical_not(has_right))
+    def _():
+        def step(k, _):
+            send_local(k)
+            return 0
+
+        lax.fori_loop(1, n_sub, step, 0)
+
+    neighbour_block(2, send_local)
+    for j in range(3, n_tiles):
         neighbour_block(j)
     for j in range(2, n_tiles):
         own_block(j)
@@ -360,6 +392,8 @@
         applied[:, at] = tile
         partial = partial + lax.dot_general(tile, tile, NT, preferred_element_type=F32)
     partial = partial * (1.0 / (panels * n_sub * n_grp))
+    store = pltpu.make_async_copy(applied, applied_out, out_s.at[0])
+    store.start()
 
     n_own = cols // 8
     stride = n_sub // n_own
@@ -434,6 +468,7 @@
         wait_for(gram_all, n_own, ga_s, ga_r).wait_recv()
 
     gram[...] = gram_all[...].reshape(cols, cols)
+    store.wait()
 
     @pl.when(owner)
     def _():
@@ -520,7 +555,10 @@
             jax.ShapeDtypeStruct((cols, cols), F32),
         ),
         in_specs=[pl.BlockSpec(memory_space=pl.ANY)] * 4,
-        out_specs=[pl.BlockSpec(memory_space=pltpu.VMEM)] * 2,
+        out_specs=[
+            pl.BlockSpec(memory_space=pl.ANY),
+            pl.BlockSpec(memory_space=pltpu.VMEM),
+        ],
         scratch_shapes=[
             pltpu.VMEM((cols, panels), BF16),
             pltpu.VMEM((4, panels), BF16),
@@ -558,6 +596,8 @@
             dma((n_grp,)), dma((n_grp,)),
             dma((1,)), dma((1,)),
             dma((4,)),
+            pltpu.VMEM((cols, panels), BF16),
+            dma((1,)),
         ],
         compiler_params=pltpu.CompilerParams(
             collective_id=0, has_side_effects=True, vmem_limit_bytes=56 << 20

time: 84 us -> 82.7 us (0.985)
  Pallas kernels: 83.2 us -> 81.9 us
    pallas_call x1, Pallas kernels: 77.4 us -> 76 us  [shards(): pl.pallas_call(functools.partial(product_kernel, n_grp, n_sub), out_shape...]
where the time goes in v5:
time: 82.7 us; the launch traced here: 82.5 us
  Pallas kernels  81.9 us (99%)
    pallas_call x1, Pallas kernels, shards(): pl.pallas_call(functools.partial(product_kernel, n_grp, n_sub), out_shape...  76 us
    pallas_call x1, Pallas kernels, shards(): pl.pallas_call(factor_kernel, out_shape=(jax.ShapeDtypeStruct((cols, pane...  5.83 us

profile of v5, /device:TPU:1, one launch (start us, length us, event | category | flops | bytes accessed | tf_op | source)
XLA Modules:
  0.0 82.5 jit_solution(4946244953569554849)
XLA Ops:
  0.6 76.0 %shard_map.59 = (bf16[128,2048]{1,0:T(8,128)(2,1)}, f32[128,128]{1,0:T(8,128)}) custom-call(bf16[128,2048]{1,0:T(8,128)(2,1)} %vec_in.1, bf16[4,2048]{1,0:T(4,128)(2,1)} %geo_in.1, f32[2,1,4,512]{3,2,1,0:T(4,128)} %tran_in.1, bf16[512,16]{1,0:T(8,128)(2,1)} %constant.2.clone.dirs_in), custom_call_target="tpu_custom_call" | custom-call | tf_op jit(solution)/shard_map/pallas_call | solution.py:551
  76.7 5.8 %shard_map.60 = (f32[128,2048]{1,0:T(8,128)}, f32[128,128]{1,0:T(8,128)}) custom-call(f32[128,128]{1,0:T(8,128)} %get-tuple-element.4.gram, bf16[128,2048]{1,0:T(8,128)(2,1)} %get-tuple-element.5.applied_in), custom_call_target="tpu_custom_call" | custom-call | tf_op jit(solution)/shard_map/pallas_call | solution.py:607

commit v6 on v5

--- a/solution.py
+++ b/solution.py
@@ -414,7 +414,7 @@
         send_block(lax.rem(mine + k, n_own))
         return 0
 
-    lax.fori_loop(1, n_own, send_gram, 0)
+    lax.fori_loop(1, n_own, send_gram, 0, unroll=True)
 
     @pl.when(jnp.logical_not(owner))
     def _():
@@ -456,7 +456,7 @@
             ).start()
             return 0
 
-        lax.fori_loop(1, n_sub, spread, 0)
+        lax.fori_loop(1, n_sub, spread, 0, unroll=True)
         for k in range(1, n_grp):
             swap(k).wait_send()
         wait_for(gram_src, n_own - 1, gr_s, gr_r).wait_send()

time: 82.7 us -> 82.6 us (level)
  no operation moved by 1% of the time
where the time goes in v6:
time: 82.6 us; the launch traced here: 82.5 us
  Pallas kernels  81.8 us (99%)
    pallas_call x1, Pallas kernels, shards(): pl.pallas_call(functools.partial(product_kernel, n_grp, n_sub), out_shape...  76 us
    pallas_call x1, Pallas kernels, shards(): pl.pallas_call(factor_kernel, out_shape=(jax.ShapeDtypeStruct((cols, pane...  5.83 us

profile of v6, /device:TPU:1, one launch (start us, length us, event | category | flops | bytes accessed | tf_op | source)
XLA Modules:
  0.0 82.5 jit_solution(3682815349031180291)
XLA Ops:
  0.6 76.0 %shard_map.59 = (bf16[128,2048]{1,0:T(8,128)(2,1)}, f32[128,128]{1,0:T(8,128)}) custom-call(bf16[128,2048]{1,0:T(8,128)(2,1)} %vec_in.1, bf16[4,2048]{1,0:T(4,128)(2,1)} %geo_in.1, f32[2,1,4,512]{3,2,1,0:T(4,128)} %tran_in.1, bf16[512,16]{1,0:T(8,128)(2,1)} %constant.2.clone.dirs_in), custom_call_target="tpu_custom_call" | custom-call | tf_op jit(solution)/shard_map/pallas_call | solution.py:551
  76.6 5.8 %shard_map.60 = (f32[128,2048]{1,0:T(8,128)}, f32[128,128]{1,0:T(8,128)}) custom-call(f32[128,128]{1,0:T(8,128)} %get-tuple-element.4.gram, bf16[128,2048]{1,0:T(8,128)(2,1)} %get-tuple-element.5.applied_in), custom_call_target="tpu_custom_call" | custom-call | tf_op jit(solution)/shard_map/pallas_call | solution.py:607
